TPU v7x, 256 devices: a whole 4x4x8 slice. The times are simulated.
256 devices in a mesh: sec: 16 (over z, y_lo), dev: 16 (over x, y_hi, core).
Axes of the slice: x: 4, y: 4 (y_hi: 2, y_lo: 2; y = y_hi * 2 + y_lo), z: 8, core: 2. Of those that a mesh axis runs over, the one named last changes fastest.
Arguments:
- latents: float32 [16, 4, 128, 128], P('sec', None, 'dev'), may hold values from -6 to 6
- noise: float32 [6, 16, 4, 128, 128], P(None, 'sec', None, 'dev'), may hold values from -6 to 6
- rewards: float32 [16], P('sec'), may hold values from -12 to 12
- prompt_ids: int32 [16], P('sec'), may hold values from 0 to 7
- context: bfloat16 [8, 77, 2048], replicated, may hold values from -6 to 6
- time_bias: float32 [6, 640], replicated, may hold values from -6 to 6
- gain_first: float32 [640], replicated, may hold values from 0.25 to 1.75
- gain_second: float32 [640], replicated, may hold values from 0.25 to 1.75
- gain_third: float32 [640], replicated, may hold values from 0.25 to 1.75
- w_in: bfloat16 [16, 640], P('sec', 'dev'), may hold values from -1.5 to 1.5
- w_conv: bfloat16 [5760, 640], P('sec', 'dev'), may hold values from -0.078125 to 0.078125
- w_query: bfloat16 [640, 640], P('sec', 'dev'), may hold values from -0.25 to 0.25
- w_key: bfloat16 [2048, 640], P('sec', 'dev'), may hold values from -0.125 to 0.125
- w_value: bfloat16 [2048, 640], P('sec', 'dev'), may hold values from -0.125 to 0.125
- w_attn_out: bfloat16 [640, 640], P('sec', 'dev'), may hold values from -0.25 to 0.25
- w_final: float32 [640, 16], P('sec', 'dev'), may hold values from -0.25 to 0.25
- moment_first: float32 [640, 16], P('sec', 'dev'), may hold values from -6 to 6
- moment_second: float32 [640, 16], P('sec', 'dev'), may hold values from 0.05 to 5
Outputs:
- final_latents: float32 [16, 4, 128, 128], P('sec', None, 'dev')
- new_final_weight: float32 [640, 16], P('sec', 'dev')
- moment_one: float32 [640, 16], P('sec', 'dev')
- moment_two: float32 [640, 16], P('sec', 'dev')
All inputs are finite; a program needn't handle non-finite values.
Results may differ from a plain program's by a relative error of at most 0.0075.
Values may be sent and summed in bfloat16 or wider, within the bound.
A program may use at most 128 MiB of HBM per device.

v0:
```python
import math

import jax
import jax.numpy as jnp
from jax import lax
from jax.sharding import PartitionSpec as P

HEAD = 64
STEPS = 6


alpha_bars = (0.1, 0.15, 0.21, 0.28, 0.36, 0.45, 0.55)
norm_eps = 1e-06
learn_rate = 0.001


def padded_2(shard, sides, width):
    for axis, dim in sides:
        size, length = (lax.axis_size(axis), shard.shape[dim])
        up = [(i, (i + 1) % size) for i in range(size - 1)]
        down = [(j, i) for i, j in up]
        last = lax.slice_in_dim(shard, length - width, length, axis=dim)
        first = lax.slice_in_dim(shard, 0, width, axis=dim)
        before = lax.ppermute(last, axis, up)
        after = lax.ppermute(first, axis, down)
        shard = jnp.concatenate([before, shard, after], axis=dim)
    return shard


def plan(step_index):
    current = alpha_bars[step_index]
    following = alpha_bars[step_index + 1]
    sigma = math.sqrt((1.0 - following) / (1.0 - current)) * math.sqrt(1.0 - current / following)
    scale = math.sqrt(following / current)
    beta = math.sqrt(1.0 - following - sigma * sigma) - scale * math.sqrt(1.0 - current)
    return (scale, beta, sigma)


def rms_scale(values, gain):
    mean_square = jnp.mean(values * values, axis=-1, keepdims=True)
    return values * lax.rsqrt(mean_square + norm_eps) * gain


def to_tokens(latent):
    batch_size, latent_chans, height, breadth = latent.shape
    blocks = latent.reshape(batch_size, latent_chans, height // 2, 2, breadth // 2, 2)
    return blocks.transpose(0, 2, 4, 1, 3, 5).reshape(
        batch_size, height // 2, breadth // 2, latent_chans * 4
    )


def from_tokens(tokens):
    batch_size, rows_here, cols_here, feature_count = tokens.shape
    blocks = tokens.reshape(batch_size, rows_here, cols_here, feature_count // 4, 2, 2)
    return blocks.transpose(0, 3, 1, 4, 2, 5).reshape(
        batch_size, feature_count // 4, 2 * rows_here, 2 * cols_here
    )


def denoise(patches, prompt_keys, prompt_values, step_bias, weights, gains):
    w_first, w_conv, w_query, w_attn_out, final_weight = weights
    batch_size, rows_here, cols_here, feature_count = patches.shape
    channels = w_first.shape[1]
    head_count = channels // HEAD
    flat_rows = batch_size * rows_here * cols_here
    hidden_in = (
        jnp.dot(
            patches.astype(jnp.bfloat16).reshape(flat_rows, feature_count),
            w_first,
            preferred_element_type=jnp.float32,
        )
        + step_bias
    )
    activated = (
        jax.nn.silu(rms_scale(hidden_in, gains[0]))
        .astype(jnp.bfloat16)
        .reshape(batch_size, rows_here, cols_here, channels)
    )
    padded = padded_2(activated, (("dev", 1),), 1)
    padded = jnp.pad(padded, ((0, 0), (0, 0), (1, 1), (0, 0)))
    columns = jnp.concatenate(
        [
            padded[:, row_off : row_off + rows_here, col_off : col_off + cols_here]
            for row_off in range(3)
            for col_off in range(3)
        ],
        axis=-1,
    )
    mixed_rows = hidden_in + jnp.dot(
        columns.reshape(flat_rows, 9 * channels), w_conv, preferred_element_type=jnp.float32
    )
    normed = rms_scale(mixed_rows, gains[1]).astype(jnp.bfloat16)
    queries = jnp.dot(normed, w_query, preferred_element_type=jnp.float32).astype(jnp.bfloat16)
    queries = queries.reshape(batch_size, rows_here * cols_here, head_count, HEAD)
    key_heads = prompt_keys.reshape(batch_size, -1, head_count, HEAD)
    value_heads = prompt_values.reshape(batch_size, -1, head_count, HEAD)
    scores = jnp.einsum(
        "bthd,bkhd->bthk", queries, key_heads, preferred_element_type=jnp.float32
    ) / math.sqrt(HEAD)
    exponent = jnp.exp(scores)
    probabilities = (exponent / jnp.sum(exponent, axis=-1, keepdims=True)).astype(jnp.bfloat16)
    attended = jnp.einsum(
        "bthk,bkhd->bthd", probabilities, value_heads, preferred_element_type=jnp.float32
    ).astype(jnp.bfloat16)
    output_rows = mixed_rows + jnp.dot(
        attended.reshape(flat_rows, channels), w_attn_out, preferred_element_type=jnp.float32
    )
    final_act = jax.nn.silu(rms_scale(output_rows, gains[2])).astype(jnp.bfloat16)
    predicted = jnp.dot(final_act, final_weight, preferred_element_type=jnp.float32)
    return (predicted.reshape(batch_size, rows_here, cols_here, feature_count), final_act)


def advantages(onehot, rewards, counts, sums, squares):
    safe_count = jnp.maximum(counts, 1.0)
    means = sums / safe_count
    spreads = jnp.sqrt(jnp.maximum(squares / safe_count - means * means, 1.0))
    own_mean = jnp.sum(onehot * means[None, :], axis=1)
    own_spread = jnp.sum(onehot * spreads[None, :], axis=1)
    return (rewards - own_mean) / own_spread


def per_device(
    latents,
    noise,
    rewards,
    prompt_ids,
    context,
    time_bias,
    gain_first,
    gain_second,
    gain_third,
    w_in,
    w_conv,
    w_query,
    w_key,
    w_value,
    w_attn_out,
    w_final,
    moment_first,
    moment_second,
):
    prompt_count = context.shape[0]
    local_images = latents.shape[0]
    total_images = local_images * lax.axis_size("sec")
    catalog = jnp.arange(prompt_count, dtype=jnp.int32)
    onehot = (prompt_ids[:, None] == catalog[None, :]).astype(jnp.float32)
    counts, sums, squares = lax.psum(
        (
            jnp.sum(onehot, axis=0),
            jnp.sum(onehot * rewards[:, None], axis=0),
            jnp.sum(onehot * (rewards * rewards)[:, None], axis=0),
        ),
        "sec",
    )
    advantage = advantages(onehot, rewards, counts, sums, squares)
    final_local = w_final.astype(jnp.bfloat16)
    selector = onehot.astype(jnp.bfloat16)
    in_rows, conv_rows, query_rows, attn_rows, final_rows, key_rows, value_rows = (
        lax.all_gather(w_in, "sec", axis=0, tiled=True),
        lax.all_gather(w_conv, "sec", axis=0, tiled=True),
        lax.all_gather(w_query, "sec", axis=0, tiled=True),
        lax.all_gather(w_attn_out, "sec", axis=0, tiled=True),
        lax.all_gather(final_local, "sec", axis=0, tiled=True),
        lax.all_gather(w_key, "sec", axis=0, tiled=True),
        lax.all_gather(w_value, "sec", axis=0, tiled=True),
    )
    in_full, conv_full, query_full, attn_full, final_full, key_full, value_full = (
        lax.all_gather(in_rows, "dev", axis=1, tiled=True),
        lax.all_gather(conv_rows, "dev", axis=1, tiled=True),
        lax.all_gather(query_rows, "dev", axis=1, tiled=True),
        lax.all_gather(attn_rows, "dev", axis=1, tiled=True),
        lax.all_gather(final_rows, "dev", axis=1, tiled=True),
        lax.all_gather(key_rows, "dev", axis=1, tiled=True),
        lax.all_gather(value_rows, "dev", axis=1, tiled=True),
    )
    own_context = jnp.einsum(
        "bp,pkf->bkf", selector, context, preferred_element_type=jnp.float32
    ).astype(jnp.bfloat16)
    own_keys = jnp.einsum(
        "bkf,fc->bkc", own_context, key_full, preferred_element_type=jnp.float32
    ).astype(jnp.bfloat16)
    own_values = jnp.einsum(
        "bkf,fc->bkc", own_context, value_full, preferred_element_type=jnp.float32
    ).astype(jnp.bfloat16)
    weights = (in_full, conv_full, query_full, attn_full, final_full)
    gains = (gain_first, gain_second, gain_third)
    channels = in_full.shape[1]
    feature_count = in_full.shape[0]
    gradient = jnp.zeros((channels, feature_count), jnp.float32)
    latent = latents
    for step_index in range(STEPS):
        scale, beta, sigma = plan(step_index)
        patches = to_tokens(latent)
        predicted, final_act = denoise(
            patches, own_keys, own_values, time_bias[step_index], weights, gains
        )
        noise_now = noise[step_index]
        noise_patch = to_tokens(noise_now).reshape(local_images, -1, feature_count)
        weighted = noise_patch * (advantage[:, None, None] * (beta / sigma))
        gradient = gradient + jnp.einsum(
            "btc,btf->cf",
            final_act.reshape(local_images, -1, channels).astype(jnp.float32),
            weighted,
            precision=lax.Precision.HIGHEST,
        )
        latent = scale * latent + beta * from_tokens(predicted) + sigma * noise_now
    sec_count = lax.axis_size("sec")
    dev_count = lax.axis_size("dev")
    row_piece = channels // sec_count
    col_piece = feature_count // dev_count
    arranged = (
        gradient.reshape(sec_count, row_piece, dev_count, col_piece)
        .transpose(0, 2, 1, 3)
        .reshape(sec_count * dev_count * row_piece, col_piece)
    )
    grad_shard = (
        -lax.psum_scatter(arranged, ("sec", "dev"), scatter_dimension=0, tiled=True) / total_images
    )
    moment_one = 0.9 * moment_first + 0.1 * grad_shard
    moment_two = 0.999 * moment_second + 0.001 * grad_shard * grad_shard
    new_weight = w_final - learn_rate * moment_one / (jnp.sqrt(moment_two) + 1e-08)
    return (latent, new_weight, moment_one, moment_two)


def solution(mesh):
    placed = (
        P("sec", None, "dev", None),
        P(None, "sec", None, "dev", None),
        P("sec"),
        P("sec"),
        P(),
        P(),
        P(),
        P(),
        P(),
        P("sec", "dev"),
        P("sec", "dev"),
        P("sec", "dev"),
        P("sec", "dev"),
        P("sec", "dev"),
        P("sec", "dev"),
        P("sec", "dev"),
        P("sec", "dev"),
        P("sec", "dev"),
    )
    return jax.shard_map(
        per_device,
        mesh=mesh,
        in_specs=placed,
        out_specs=(P("sec", None, "dev", None), P("sec", "dev"), P("sec", "dev"), P("sec", "dev")),
        check_vma=False,
    )
```

profile of v0, /device:TPU:1, one launch (start us, length us, event | category | flops | bytes accessed | tf_op | source)
XLA Modules:
  0.0 608.3 jit_solution(9156863310815345228)
XLA Ops:
  7.3 33.6 %all_gather.46 = bf16[2048,40]{0,1:T(8,128)(2,1)} all-gather(bf16[128,40]{0,1:T(8,128)(2,1)} %param.31), channel_id=1, replica_groups=mesh['sec'=16,'dev'=16] {'sec'}, dimensions={0}, use_global_device_ids=true | all-gather | bytes 174080 | tf_op jit(solution)/shard_map/all_gather | solution.py:165
  41.0 26.5 %all_gather.48 = bf16[2048,40]{0,1:T(8,128)(2,1)} all-gather(bf16[128,40]{0,1:T(8,128)(2,1)} %param.30), channel_id=1, replica_groups=mesh['sec'=16,'dev'=16] {'sec'}, dimensions={0}, use_global_device_ids=true | all-gather | bytes 174080 | tf_op jit(solution)/shard_map/all_gather | solution.py:164
  67.5 28.3 %all-gather.2 = bf16[16,360,40]{1,2,0:T(8,128)(2,1)S(1)} all-gather(bf16[1,360,40]{1,2,0:T(8,128)(2,1)} %bitcast.503), channel_id=1, replica_groups=mesh['sec'=16,'dev'=16] {'sec'}, dimensions={0}, use_global_device_ids=true | all-gather | bytes 489600 | tf_op jit(solution)/shard_map/all_gather | solution.py:160
  99.0 23.8 %all-gather = bf16[16,1,40]{2,1,0:T(2,128)(2,1)S(1)} all-gather(bf16[1,1,40]{2,1,0:T(2,128)(2,1)S(1)} %bitcast.505), channel_id=1, replica_groups=mesh['sec'=16,'dev'=16] {'sec'}, dimensions={0}, use_global_device_ids=true | all-gather | bytes 1360 | tf_op jit(solution)/shard_map/all_gather | solution.py:159
  122.8 51.1 %all-gather.1 = bf16[16,40,16]{1,2,0:T(8,128)(2,1)S(1)} all-gather(bf16[1,40,16]{1,2,0:T(8,128)(2,1)S(1)} %bitcast.504), channel_id=1, replica_groups=mesh['sec'=16,'dev'=16] {'dev'}, dimensions={0}, use_global_device_ids=true | all-gather | bytes 21760 | tf_op jit(solution)/shard_map/all_gather | solution.py:168
  184.3 25.5 %all-reduce.8 = (f32[8]{0:T(128)S(1)}, f32[8]{0:T(128)S(1)}, f32[8]{0:T(128)S(1)}) all-reduce(f32[8]{0:T(128)S(1)} %get-tuple-element.149, f32[8]{0:T(128)S(1)} %fusion.42, f32[8]{0:T(128)S(1)} %get-tuple-element.148), channel_id=1, replica_groups=mesh['sec'=16,'dev'=16] {'sec'}, use_global_device_ids=true, to_apply=%region_24.25 | all-reduce | flops 24 | bytes 192 | tf_op jit(solution)/shard_map/psum | solution.py:147
  211.8 25.3 %all_gather.50 = bf16[640,40]{1,0:T(8,128)(2,1)S(1)} all-gather(bf16[40,40]{1,0:T(8,128)(2,1)S(1)} %copy-done.37), channel_id=1, replica_groups=mesh['sec'=16,'dev'=16] {'sec'}, dimensions={0}, use_global_device_ids=true | all-gather | bytes 54400 | tf_op jit(solution)/shard_map/all_gather | solution.py:161
  237.2 24.8 %all_gather.52 = bf16[640,40]{1,0:T(8,128)(2,1)S(1)} all-gather(bf16[40,40]{1,0:T(8,128)(2,1)S(1)} %copy-done.38), channel_id=1, replica_groups=mesh['sec'=16,'dev'=16] {'sec'}, dimensions={0}, use_global_device_ids=true | all-gather | bytes 54400 | tf_op jit(solution)/shard_map/all_gather | solution.py:162
  265.1 44.0 %all_gather.53 = bf16[640,640]{0,1:T(8,128)(2,1)S(1)} all-gather(bf16[640,40]{0,1:T(8,128)(2,1)S(1)} %copy-done.11), channel_id=1, replica_groups=mesh['sec'=16,'dev'=16] {'dev'}, dimensions={1}, use_global_device_ids=true | all-gather | bytes 870400 | tf_op jit(solution)/shard_map/all_gather | solution.py:171
  309.0 23.1 %all_gather.51 = bf16[640,640]{0,1:T(8,128)(2,1)S(1)} all-gather(bf16[640,40]{0,1:T(8,128)(2,1)S(1)} %copy.174), channel_id=1, replica_groups=mesh['sec'=16,'dev'=16] {'dev'}, dimensions={1}, use_global_device_ids=true | all-gather | bytes 870400 | tf_op jit(solution)/shard_map/all_gather | solution.py:170
  333.7 23.7 %all-reduce.6 = bf16[640]{0:T(1024)(128)(2,1)S(1)} all-reduce(bf16[640]{0:T(1024)(128)(2,1)S(1)} %dynamic-update-slice), channel_id=1, replica_groups=mesh['sec'=16,'dev'=16] {'sec'}, use_global_device_ids=true, to_apply=%add.6 | all-reduce | flops 640 | bytes 2560
  357.4 28.3 %all-gather.3 = bf16[16,1,640]{2,1,0:T(2,128)(2,1)S(1)} all-gather(bf16[1,1,640]{2,1,0:T(2,128)(2,1)S(1)} %reshape.829), channel_id=1, replica_groups=mesh['sec'=16,'dev'=16] {'dev'}, dimensions={0}, use_global_device_ids=true | all-gather | bytes 21760 | tf_op jit(solution)/shard_map/all_gather | solution.py:172
  409.4 6.6 %multiply_reduce_fusion.16 = (f32[256]{0:T(256)S(1)}, f32[256,640]{1,0:T(8,128)S(1)}) fusion(f32[256,640]{1,0:T(8,128)S(1)} %copy-done.3, bf16[256,5760]{1,0:T(8,128)(2,1)} %constant_dynamic-update-slice_fusion, bf16[5760,640]{0,1:T(8,128)(2,1)} %all-gather.8.cloned.1.call-done), kind=kOutput, calls=%fused_computation.104 | convolution fusion | flops 1887928064 | bytes 11633664 | tf_op jit(solution)/shard_map/dot_general | solution.py:89
  420.3 3.6 collective-permute-start.2
  427.0 4.2 collective-permute-done.3
  432.3 5.7 multiply_reduce_fusion.13
  448.8 3.3 collective-permute-done.5
  453.3 5.7 multiply_reduce_fusion.10
  468.9 3.6 collective-permute-done.7
  473.6 5.7 multiply_reduce_fusion.7
  490.3 3.3 collective-permute-done.9
  508.7 3.8 collective-permute-done.11
  513.7 5.7 multiply_reduce_fusion.1
  524.1 75.7 %all-reduce.7 = f32[10240,1]{0,1:T(1,128)S(1)} all-reduce(f32[10240,1]{0,1:T(1,128)S(1)} %reshape.819), channel_id=2, replica_groups=mesh['sec'=16,'dev'=16] {'sec','dev'}, use_global_device_ids=true, to_apply=%region_29.30.clone | all-reduce | flops 10240 | bytes 81920
  (371 shorter events, 104.6 us)
Async XLA Ops:
  7.2 256.2 %copy-start = (bf16[8,77,2048]{2,0,1:T(8,128)(2,1)S(1)}, bf16[8,77,2048]{2,0,1:T(8,128)(2,1)}, u32[]{:S(2)}) copy-start(bf16[8,77,2048]{2,0,1:T(8,128)(2,1)} %param.22) | copy-start | bytes 7569412
  7.2 167.3 %copy-start.36 = (f32[6,640]{1,0:T(8,128)S(1)}, f32[6,640]{1,0:T(8,128)}, u32[]{:S(2)}) copy-start(f32[6,640]{1,0:T(8,128)} %param.23) | copy-start | bytes 46084
  7.2 169.2 %copy-start.10 = (f32[640]{0:T(1024)S(1)}, f32[640]{0:T(1024)}, u32[]{:S(2)}) copy-start(f32[640]{0:T(1024)} %param.24) | copy-start | bytes 7684
  7.2 395.8 %all-gather.10.cloned.1.call-start = ((), (), s32[]{:S(2)}) async-start(), calls=%async_computation.1 | async-start | bytes 2785280 | tf_op jit(solution)/shard_map/all_gather | solution.py:174
  40.9 365.6 %all-gather.12.cloned.1.call-start = ((), (), s32[]{:S(2)}) async-start(), calls=%async_computation.2 | async-start | bytes 2785280 | tf_op jit(solution)/shard_map/all_gather | solution.py:173
  67.5 341.9 %all-gather.8.cloned.1.call-start = ((), (), s32[]{:S(2)}) async-start(), calls=%async_computation | async-start | bytes 7833600 | tf_op jit(solution)/shard_map/all_gather | solution.py:169
  67.5 144.2 %copy-start.37 = (bf16[40,40]{1,0:T(8,128)(2,1)S(1)}, bf16[40,40]{1,0:T(8,128)(2,1)}, u32[]{:S(2)}) copy-start(bf16[40,40]{1,0:T(8,128)(2,1)} %param.29) | copy-start | bytes 9604
  95.8 141.4 %copy-start.38 = (bf16[40,40]{1,0:T(8,128)(2,1)S(1)}, bf16[40,40]{1,0:T(8,128)(2,1)}, u32[]{:S(2)}) copy-start(bf16[40,40]{1,0:T(8,128)(2,1)} %param.32) | copy-start | bytes 9604
  95.8 166.9 %copy-start.9 = (f32[6,1,4,8,128]{4,3,2,1,0:T(8,128)S(1)}, f32[6,1,4,8,128]{4,3,2,1,0:T(8,128)}, u32[]{:S(2)}) copy-start(f32[6,1,4,8,128]{4,3,2,1,0:T(8,128)} %param.19) | copy-start | bytes 294916
  178.0 215.2 %collective-permute-start = (bf16[1,1,64,640]{3,2,1,0:T(8,128)(2,1)}, bf16[1,1,64,640]{3,2,1,0:T(8,128)(2,1)}, u32[]{:S(2)}, u32[]{:S(2)}) collective-permute-start(bf16[1,1,64,640]{3,2,1,0:T(8,128)(2,1)} %get-tuple-element.92), channel_id=1, source_target_pairs={{0,1},{1,2},{2,3},{3,4},{4,5},{5,6},{6,7},{7,8},{8,9},{9,10},{10,1... | collective-permute-start | bytes 245768 | tf_op jit(solution)/shard_map/ppermute | solution.py:24
  180.0 213.3 %collective-permute-start.1 = (bf16[1,1,64,640]{3,2,1,0:T(8,128)(2,1)}, bf16[1,1,64,640]{3,2,1,0:T(8,128)(2,1)}, u32[]{:S(2)}, u32[]{:S(2)}) collective-permute-start(bf16[1,1,64,640]{3,2,1,0:T(8,128)(2,1)} %get-tuple-element.93), channel_id=1, source_target_pairs={{1,0},{2,1},{3,2},{4,3},{5,4},{6,5},{7,6},{8,7},{9,8},{10,9},{11,1... | collective-permute-start | bytes 245768 | tf_op jit(solution)/shard_map/ppermute | solution.py:25
  265.0 122.5 %copy-start.30 = (f32[1,1,4,8,128]{4,3,2,1,0:T(8,128)S(1)}, f32[1,1,4,8,128]{4,3,2,1,0:T(8,128)}, u32[]{:S(2)}) copy-start(f32[1,1,4,8,128]{4,3,2,1,0:T(8,128)} %get-tuple-element.95) | copy-start | bytes 49156
  265.0 123.6 %copy-start.29 = (f32[1,1,4,8,128]{4,3,2,1,0:T(8,128)S(1)}, f32[1,1,4,8,128]{4,3,2,1,0:T(8,128)}, u32[]{:S(2)}) copy-start(f32[1,1,4,8,128]{4,3,2,1,0:T(8,128)} %get-tuple-element.96) | copy-start | bytes 49156
  265.0 124.8 %copy-start.28 = (f32[1,1,4,8,128]{4,3,2,1,0:T(8,128)S(1)}, f32[1,1,4,8,128]{4,3,2,1,0:T(8,128)}, u32[]{:S(2)}) copy-start(f32[1,1,4,8,128]{4,3,2,1,0:T(8,128)} %get-tuple-element.97) | copy-start | bytes 49156
  420.3 6.7 %collective-permute-start.2 = (bf16[1,1,64,640]{3,2,1,0:T(8,128)(2,1)S(1)}, bf16[1,1,64,640]{3,2,1,0:T(8,128)(2,1)S(1)}, u32[]{:S(2)}, u32[]{:S(2)}) collective-permute-start(bf16[1,1,64,640]{3,2,1,0:T(8,128)(2,1)S(1)} %get-tuple-element.88), channel_id=1, source_target_pairs={{0,1},{1,2},{2,3},{3,4},{4,5},{5,6},{6,7},{7,8},{8,9},{9,10},{10,1... | collective-permute-start | bytes 245768 | tf_op jit(solution)/shard_map/ppermute | solution.py:24
  423.9 7.3 %collective-permute-start.3 = (bf16[1,1,64,640]{3,2,1,0:T(8,128)(2,1)S(1)}, bf16[1,1,64,640]{3,2,1,0:T(8,128)(2,1)S(1)}, u32[]{:S(2)}, u32[]{:S(2)}) collective-permute-start(bf16[1,1,64,640]{3,2,1,0:T(8,128)(2,1)S(1)} %get-tuple-element.89), channel_id=1, source_target_pairs={{1,0},{2,1},{3,2},{4,3},{5,4},{6,5},{7,6},{8,7},{9,8},{10,9},{11,1... | collective-permute-start | bytes 245768 | tf_op jit(solution)/shard_map/ppermute | solution.py:25
  442.9 5.9 collective-permute-start.4
  444.8 7.3 %collective-permute-start.5 = (bf16[1,1,64,640]{3,2,1,0:T(8,128)(2,1)S(1)}, bf16[1,1,64,640]{3,2,1,0:T(8,128)(2,1)S(1)}, u32[]{:S(2)}, u32[]{:S(2)}) collective-permute-start(bf16[1,1,64,640]{3,2,1,0:T(8,128)(2,1)S(1)} %get-tuple-element.85), channel_id=1, source_target_pairs={{1,0},{2,1},{3,2},{4,3},{5,4},{6,5},{7,6},{8,7},{9,8},{10,9},{11,1... | collective-permute-start | bytes 245768 | tf_op jit(solution)/shard_map/ppermute | solution.py:25
  463.3 5.6 collective-permute-start.6
  465.2 7.3 %collective-permute-start.7 = (bf16[1,1,64,640]{3,2,1,0:T(8,128)(2,1)S(1)}, bf16[1,1,64,640]{3,2,1,0:T(8,128)(2,1)S(1)}, u32[]{:S(2)}, u32[]{:S(2)}) collective-permute-start(bf16[1,1,64,640]{3,2,1,0:T(8,128)(2,1)S(1)} %get-tuple-element.81), channel_id=1, source_target_pairs={{1,0},{2,1},{3,2},{4,3},{5,4},{6,5},{7,6},{8,7},{9,8},{10,9},{11,1... | collective-permute-start | bytes 245768 | tf_op jit(solution)/shard_map/ppermute | solution.py:25
  484.2 6.1 collective-permute-start.8
  486.3 7.3 %collective-permute-start.9 = (bf16[1,1,64,640]{3,2,1,0:T(8,128)(2,1)S(1)}, bf16[1,1,64,640]{3,2,1,0:T(8,128)(2,1)S(1)}, u32[]{:S(2)}, u32[]{:S(2)}) collective-permute-start(bf16[1,1,64,640]{3,2,1,0:T(8,128)(2,1)S(1)} %get-tuple-element.77), channel_id=1, source_target_pairs={{1,0},{2,1},{3,2},{4,3},{5,4},{6,5},{7,6},{8,7},{9,8},{10,9},{11,1... | collective-permute-start | bytes 245768 | tf_op jit(solution)/shard_map/ppermute | solution.py:25
  502.5 6.2 %collective-permute-start.10 = (bf16[1,1,64,640]{3,2,1,0:T(8,128)(2,1)S(1)}, bf16[1,1,64,640]{3,2,1,0:T(8,128)(2,1)S(1)}, u32[]{:S(2)}, u32[]{:S(2)}) collective-permute-start(bf16[1,1,64,640]{3,2,1,0:T(8,128)(2,1)S(1)} %get-tuple-element.72), channel_id=1, source_target_pairs={{0,1},{1,2},{2,3},{3,4},{4,5},{5,6},{6,7},{7,8},{8,9},{9,10},{10,1... | collective-permute-start | bytes 245768 | tf_op jit(solution)/shard_map/ppermute | solution.py:24
  504.4 8.1 %collective-permute-start.11 = (bf16[1,1,64,640]{3,2,1,0:T(8,128)(2,1)S(1)}, bf16[1,1,64,640]{3,2,1,0:T(8,128)(2,1)S(1)}, u32[]{:S(2)}, u32[]{:S(2)}) collective-permute-start(bf16[1,1,64,640]{3,2,1,0:T(8,128)(2,1)S(1)} %get-tuple-element.73), channel_id=1, source_target_pairs={{1,0},{2,1},{3,2},{4,3},{5,4},{6,5},{7,6},{8,7},{9,8},{10,9},{11,1... | collective-permute-start | bytes 245768 | tf_op jit(solution)/shard_map/ppermute | solution.py:25
  (40 other events, 1102.4 us)
Sparse Core Ops, SparseCore 0:
  41.0 63.9 all-gather.9
  107.7 54.0 all-gather.11
  164.6 74.5 all-gather.7
where the time goes:
time: 614 us; the launch traced here: 608 us
  blocking collectives  434 us (71%)
  matrix products  60.3 us (10%)
  local copies, waits for them, and re-layouts  36 us (6%)
  starting transfers between devices  28.7 us (5%)
  between operations  19 us (3%)
  waiting for transfers between devices  18.2 us (3%)
  other arithmetic  12.7 us (2%)
    unnamed x2, blocking collectives  99.3 us
    all_gather x1, blocking collectives, per_device(): lax.all_gather(in_rows, 'dev', axis=1, tiled=True)  51.1 us
    all_gather x1, blocking collectives, per_device(): lax.all_gather(attn_rows, 'dev', axis=1, tiled=True)  44 us
    all_gather x1, blocking collectives, per_device(): lax.all_gather(w_value, 'sec', axis=0, tiled=True)  33.6 us
    dot_general x6, matrix products, denoise(): jnp.dot(columns.reshape(flat_rows, 9 * channels), w_conv, preferred_eleme...  32.1 us
    all_gather x1, blocking collectives, per_device(): lax.all_gather(w_conv, 'sec', axis=0, tiled=True)  28.3 us
    all_gather x1, blocking collectives, per_device(): lax.all_gather(final_rows, 'dev', axis=1, tiled=True)  28.3 us
    all_gather x1, blocking collectives, per_device(): lax.all_gather(w_key, 'sec', axis=0, tiled=True)  26.5 us
  transfers between devices with their start and end apart: 15, of which 5 were waited for; matrix products, arithmetic and copies ran while one was open for 7% of the time, Pallas kernels for 0%

commit v1 on v0

v1 whole, which is shorter than its diff:
```python
import math

import jax
import jax.numpy as jnp
from jax import lax
from jax.experimental import pallas as pl
from jax.experimental.pallas import tpu as pltpu
from jax.sharding import PartitionSpec as P

HEAD = 64
STEPS = 6
ROWS = 4
COLS = 64
TOK = ROWS * COLS
C = 640
FEAT = 16
PAIRS = C // (2 * HEAD)
SHARD = 40
CONV_ROWS = 360
LANES = 512
FINAL_AT = 384
QUERY_AT = 400
OUT_AT = 440
IN_AT = 480
CTX_TOK = 77

alpha_bars = (0.1, 0.15, 0.21, 0.28, 0.36, 0.45, 0.55)
norm_eps = 1e-06
learn_rate = 0.001
NX, NY, NZ = 4, 4, 8
SIZE = {"x": NX, "y": NY, "z": NZ}
CLASSES = (
    ((0, 16), "yzx"),
    ((16, 32), "xzy"),
    ((32, 40), "xyz"),
)
MESH_ID = pl.DeviceIdType.MESH
F32 = jnp.float32
BF16 = jnp.bfloat16


def plan(step_index):
    current = alpha_bars[step_index]
    following = alpha_bars[step_index + 1]
    sigma = math.sqrt((1.0 - following) / (1.0 - current)) * math.sqrt(1.0 - current / following)
    scale = math.sqrt(following / current)
    beta = math.sqrt(1.0 - following - sigma * sigma) - scale * math.sqrt(1.0 - current)
    return (scale, beta, sigma)


PLANS = [plan(i) for i in range(STEPS)]


def dot(a, b):
    return jnp.dot(a, b, preferred_element_type=F32)


def dot_t(a, b):
    return lax.dot_general(a, b, (((1,), (1,)), ((), ())), preferred_element_type=F32)


def rms(values, gain):
    mean_square = jnp.mean(values * values, axis=-1, keepdims=True)
    return values * lax.rsqrt(mean_square + norm_eps) * gain


def silu(v):
    half = 0.5 * v
    return half + half * jnp.tanh(half)


def choose(index, values):
    out = jnp.float32(values[0])
    for i in range(1, len(values)):
        out = jnp.where(index == i, jnp.float32(values[i]), out)
    return out


def iota(shape, dim):
    return lax.broadcasted_iota(jnp.int32, shape, dim)


def body(
    lat_ref,
    noise_ref,
    reward_ref,
    prompt_ref,
    ctx_ref,
    bias_ref,
    g1_ref,
    g2_ref,
    g3_ref,
    w_in_ref,
    w_conv_ref,
    w_query_ref,
    w_key_ref,
    w_value_ref,
    w_out_ref,
    w_final_ref,
    m1_ref,
    m2_ref,
    x_out,
    w_new_out,
    m1_out,
    m2_out,
    G,
    KG,
    KT,
    SA,
    Wc,
    Wq,
    Wo,
    Win,
    WF,
    Kbd,
    Vbd,
    PB,
    A,
    H,
    M,
    X,
    NZT,
    NTS,
    FA,
    GA,
    GS,
    GR,
    R1,
    RR,
    g_send,
    g_recv,
    b_send,
    b_recv,
    k_send,
    k_recv,
    t_send,
    t_recv,
    h_send,
    h_recv,
    r_send,
    r_recv,
    s_send,
    s_recv,
):
    sec = lax.axis_index("sec")
    dev = lax.axis_index("dev")
    z, ylo = sec // 2, sec % 2
    xx, yhi, core = dev // 4, (dev // 2) % 2, dev % 2
    yy = yhi * 2 + ylo
    me = {"x": xx, "y": yy, "z": z}

    def device(x, y, zc, c):
        return (zc * 2 + y % 2, x * 4 + (y // 2) * 2 + c)

    def neighbour(axis, delta):
        pos = dict(me)
        pos[axis] = lax.rem(me[axis] + delta + SIZE[axis], SIZE[axis])
        return device(pos["x"], pos["y"], pos["z"], core)

    barrier = pltpu.get_barrier_semaphore()
    cross_y = (sec - 2 * ylo + 1, dev - 2 * yhi + 2 * (1 - yhi))
    for k in range(1, 16):
        pl.semaphore_signal(barrier, inc=1, device_id=(lax.rem(sec + k, 16), dev), device_id_type=MESH_ID)
        pl.semaphore_signal(barrier, inc=1, device_id=(sec, lax.rem(dev + k, 16)), device_id_type=MESH_ID)
    pl.semaphore_signal(barrier, inc=1, device_id=cross_y, device_id_type=MESH_ID)

    eye = (iota((SHARD, SHARD), 0) == iota((SHARD, SHARD), 1)).astype(BF16)
    SA[...] = jnp.zeros_like(SA)
    SA[0:CONV_ROWS, :] = w_conv_ref[...].astype(F32)
    SA[QUERY_AT : QUERY_AT + SHARD, :] = w_query_ref[...].astype(F32)
    SA[OUT_AT : OUT_AT + SHARD, :] = w_out_ref[...].astype(F32)
    SA[IN_AT : IN_AT + 1, :] = w_in_ref[...].astype(F32)
    block = dot_t(eye, SA[...].astype(BF16))
    w_fin = jnp.broadcast_to(w_final_ref[...], (SHARD, LANES))
    block = jnp.where(iota((SHARD, LANES), 1) == FINAL_AT + dev, w_fin, block)
    G[z, ylo, xx, yhi, core] = block.astype(BF16)

    KG[sec, 0:SHARD, :] = dot_t(eye, w_key_ref[...]).astype(BF16)
    KG[sec, SHARD : 2 * SHARD, :] = dot_t(eye, w_value_ref[...]).astype(BF16)
    reward = jnp.broadcast_to(reward_ref[...], (8, 128))
    prompt = jnp.broadcast_to(prompt_ref[...].astype(F32), (8, 128))
    hi = reward.astype(BF16).astype(F32)
    mid = (reward - hi).astype(BF16).astype(F32)
    low = reward - hi - mid
    lane8 = iota((8, 128), 1)
    stats = jnp.where(lane8 == 0, prompt, 0.0)
    for i, part in enumerate((hi, mid, low)):
        stats = jnp.where(lane8 == i + 1, part, stats)
    KG[sec, 80:88, :] = stats.astype(BF16)

    def turn(rows16):
        wide = jnp.concatenate([rows16, jnp.zeros((128 - FEAT, TOK), F32)], axis=0)
        return jnp.transpose(wide)

    X[...] = turn(lat_ref[...])
    PB[0, COLS : COLS + TOK, :] = X[...].astype(BF16)

    pl.semaphore_wait(barrier, 31)

    def halo_copy(t, up):
        if up:
            src, dst, to, i = PB.at[t, pl.ds(COLS, COLS)], PB.at[t, pl.ds(COLS + TOK, COLS)], dev - 1, 0
        else:
            src, dst, to, i = PB.at[t, pl.ds(TOK, COLS)], PB.at[t, pl.ds(0, COLS)], dev + 1, 1
        return pltpu.make_async_remote_copy(
            src, dst, h_send.at[t, i], h_recv.at[t, i], device_id=(sec, to), device_id_type=MESH_ID
        )

    def start_halo(t):
        @pl.when(dev > 0)
        def _():
            halo_copy(t, True).start()

        @pl.when(dev < 15)
        def _():
            halo_copy(t, False).start()

    def wait_halo(t):
        @pl.when(dev > 0)
        def _():
            halo_copy(t, True).wait_send()
            halo_copy(t, False).wait_recv()

        @pl.when(dev < 15)
        def _():
            halo_copy(t, False).wait_send()
            halo_copy(t, True).wait_recv()

    start_halo(0)

    def to_peer(src, dst, send, recv, peer):
        return pltpu.make_async_remote_copy(src, dst, send, recv, device_id=peer, device_id_type=MESH_ID)

    def key_copy(k):
        return to_peer(KG.at[sec], KG.at[sec], k_send.at[k], k_recv.at[k], (lax.rem(sec + k, 16), dev))

    for k in range(1, 16):
        key_copy(k).start()

    pushes = []

    def region(known, axis, origin, rows, half):
        index = {}
        for a in "xyz":
            if a == axis:
                index[a] = origin
            elif a in known:
                index[a] = None
            else:
                index[a] = me[a]
        lanes = pl.ds(0, LANES) if half is None else pl.ds(half * (LANES // 2), LANES // 2)
        zi = pl.ds(0, NZ) if index["z"] is None else index["z"]
        xi = pl.ds(0, NX) if index["x"] is None else index["x"]
        if index["y"] is None:
            lo_i, hi_i = pl.ds(0, 2), pl.ds(0, 2)
        else:
            lo_i, hi_i = index["y"] % 2, index["y"] // 2
        return G.at[zi, lo_i, xi, hi_i, core, pl.ds(rows[0], rows[1] - rows[0]), lanes]

    def gather(k, rows, order):
        for stage, axis in enumerate(order):
            n, known = SIZE[axis], order[:stage]
            last = stage == 2

            def copy(direction, r):
                step = 1 if direction == 0 else -1
                origin = lax.rem(me[axis] - step * (r - 1) + n, n)
                half = direction if r == n // 2 else None
                ref = region(known, axis, origin, rows, half)
                return to_peer(
                    ref, ref, g_send.at[k, stage, direction, r - 1], g_recv.at[k, stage, direction, r - 1], neighbour(axis, step)
                )

            def push(origin):
                ref = region(known, axis, lax.rem(origin + n, n), rows, None)
                i = len(pushes)
                c = to_peer(ref, ref, b_send.at[i], b_recv.at[i], (sec, dev + 1 - 2 * core))
                c.start()
                pushes.append(c)

            for r in range(1, n // 2 + 1):
                for direction in (0, 1):
                    if r > 1:
                        copy(direction, r - 1).wait_recv()
                    copy(direction, r).start()
                if last:
                    if r == 1:
                        push(me[axis])
                    else:
                        push(me[axis] - (r - 1))
                        push(me[axis] + (r - 1))
                yield
            for direction in (0, 1):
                copy(direction, n // 2).wait_recv()
            if last:
                push(me[axis] + n // 2)
            for r in range(1, n // 2 + 1):
                for direction in (0, 1):
                    copy(direction, r).wait_send()

    def keys_and_values():
        for k in range(1, 16):
            key_copy(k).wait()
        yield
        wide = jnp.concatenate([KG[s, 0:80, :] for s in range(16)], axis=1)
        own = dot_t(wide, ctx_ref[...])
        KT[dev] = jnp.zeros_like(KT[dev])
        KT[dev, :, 0:80] = own.astype(BF16)

        def copy(k):
            return to_peer(KT.at[dev], KT.at[dev], t_send.at[k], t_recv.at[k], (sec, lax.rem(dev + k, 16)))

        for k in range(1, 16):
            copy(k).start()
        yield
        yield
        yield
        for k in range(1, 16):
            copy(k).wait()
        kt = jnp.concatenate([KT[d, 0:SHARD, :] for d in range(16)], axis=0)
        vt = jnp.concatenate([KT[d, SHARD : 2 * SHARD, :] for d in range(16)], axis=0)
        v = jnp.transpose(vt.astype(F32))
        row = iota((128, 128), 0)
        lane = iota((128, 128), 1)
        for p in range(PAIRS):
            part = kt[128 * p : 128 * (p + 1), :].astype(F32) * (1.0 / math.sqrt(HEAD))
            Kbd[p, :, 0:128] = jnp.where(row < HEAD, part, 0.0).astype(BF16)
            Kbd[p, :, 128:256] = jnp.where(row < HEAD, 0.0, part).astype(BF16)
            part = v[:, 128 * p : 128 * (p + 1)]
            Vbd[p, 0:128, :] = jnp.where(lane < HEAD, part, 0.0).astype(BF16)
            Vbd[p, 128:256, :] = jnp.where(lane < HEAD, 0.0, part).astype(BF16)

    def split_noise():
        for t in range(STEPS):
            nt = noise_ref[t]
            NZT[t] = turn(nt)
            top = nt.astype(BF16)
            NTS[t, 0:FEAT, :] = top
            NTS[t, FEAT : 2 * FEAT, :] = (nt - top.astype(F32)).astype(BF16)
        yield

    running = [gather(k, rows, order) for k, (rows, order) in enumerate(CLASSES)]
    running += [keys_and_values(), split_noise()]
    while running:
        left = []
        for g in running:
            try:
                next(g)
                left.append(g)
            except StopIteration:
                pass
        running = left
    for c in pushes:
        c.wait()

    Win[...] = jnp.zeros_like(Win)
    lane_w = iota((SHARD, 128), 1)

    def settle(zi, carry):
        turned = []
        for lo in range(2):
            parts = G[zi, lo].astype(F32)
            flat = parts.reshape(C, LANES)
            tail = jnp.sum(parts.reshape(16, SHARD, LANES)[:, :, FINAL_AT:LANES], axis=0)
            WF[zi, lo] = jnp.where(lane_w < FEAT, tail, 0.0)
            turned.append(jnp.transpose(flat))
        conv = jnp.concatenate([w[0:CONV_ROWS] for w in turned], axis=0).astype(BF16)
        Wc[pl.ds(pl.multiple_of(zi * 2 * CONV_ROWS, 16), 2 * CONV_ROWS), :] = conv
        at = pl.ds(pl.multiple_of(zi * 2 * SHARD, 16), 2 * SHARD)
        Wq[at, :] = jnp.concatenate([w[QUERY_AT : QUERY_AT + SHARD] for w in turned], axis=0).astype(BF16)
        Wo[at, :] = jnp.concatenate([w[OUT_AT : OUT_AT + SHARD] for w in turned], axis=0).astype(BF16)
        for lo in range(2):
            Win[pl.ds(zi * 2 + lo, 1), :] = turned[lo][IN_AT : IN_AT + 1]
        return carry

    lax.fori_loop(0, NZ, settle, 0)

    token_col = iota((TOK, C), 0) % COLS
    tok_row = iota((2 * HEAD * 2, 2 * HEAD * 2), 0)
    tok_col = iota((2 * HEAD * 2, 2 * HEAD * 2), 1)
    ones = (((tok_row < 128) == (tok_col < 128)) & (tok_row % 128 < CTX_TOK)).astype(BF16)
    GA[...] = jnp.zeros_like(GA)

    def spread(act, at, n):
        col = iota((n, C), 0) % COLS
        rows = pl.ds(at, n)
        A[rows, C : 2 * C] = act.astype(BF16)
        A[rows, 0:C] = jnp.where(col == 0, 0.0, pltpu.roll(act, 1, 0)).astype(BF16)
        A[rows, 2 * C : 3 * C] = jnp.where(col == COLS - 1, 0.0, pltpu.roll(act, n - 1, 0)).astype(BF16)

    def denoise(t, carry):
        scale = choose(t, [p[0] for p in PLANS])
        beta = choose(t, [p[1] for p in PLANS])
        sigma = choose(t, [p[2] for p in PLANS])
        weight = choose(t, [p[1] / p[2] for p in PLANS])
        bias = bias_ref[pl.ds(t, 1), :]
        w_first = Win[...].astype(BF16)
        hidden = dot(PB[t, COLS : COLS + TOK, :], w_first) + bias
        H[...] = hidden
        spread(silu(rms(hidden, g1_ref[...])), COLS, TOK)
        M[...] = H[...] + dot(A[COLS : COLS + TOK, :], Wc[3 * C : 6 * C, :])
        wait_halo(t)
        edge = jnp.concatenate([PB[t, 0:COLS, :], PB[t, COLS + TOK :, :]], axis=0)
        act = silu(rms(dot(edge, w_first) + bias, g1_ref[...]))
        above = jnp.where(dev > 0, act[0:COLS], 0.0)
        below = jnp.where(dev < 15, act[COLS:], 0.0)
        spread(above, 0, COLS)
        spread(below, COLS + TOK, COLS)
        M[...] += dot(A[0:TOK, :], Wc[0 : 3 * C, :])
        M[...] += dot(A[2 * COLS : 2 * COLS + TOK, :], Wc[6 * C : 9 * C, :])

        def finish(ranges):
            def load(ref, *lead):
                return jnp.concatenate([ref[(*lead, slice(a, b))] for a, b in ranges], axis=0)

            mixed = load(M)
            normed = rms(mixed, g2_ref[...]).astype(BF16)
            queries = dot(normed, Wq[...]).astype(BF16)
            heads = []
            for p in range(PAIRS):
                e = jnp.exp(dot(queries[:, 128 * p : 128 * (p + 1)], Kbd[p]))
                total = dot(e.astype(BF16), ones)
                heads.append(dot((e * (1.0 / total)).astype(BF16), Vbd[p]).astype(BF16))
            out = mixed + dot(jnp.concatenate(heads, axis=1), Wo[...])
            final = silu(rms(out, g3_ref[...])).astype(BF16)
            w_last = WF[...].reshape(C, 128).astype(BF16)
            x_new = scale * load(X) + beta * dot(final, w_last) + sigma * load(NZT, t)
            at = 0
            for a, b in ranges:
                n = b - a
                FA[a:b, :] = final[at : at + n]
                X[a:b, :] = x_new[at : at + n]
                PB[t + 1, a + COLS : b + COLS, :] = x_new[at : at + n].astype(BF16)
                at += n

        finish(((0, COLS), (TOK - COLS, TOK)))

        @pl.when(t < STEPS - 1)
        def _():
            start_halo(t + 1)

        finish(((COLS, TOK - COLS),))
        GA[...] += weight * dot(NTS[t], FA[...])
        return carry

    lax.fori_loop(0, STEPS, denoise, 0)

    x_out[...] = jnp.transpose(X[...])[0:FEAT]

    table = jnp.concatenate([KG[s, 80:88, :].astype(F32)[0:1] for s in range(16)], axis=0)
    ids = table[:, 0:1]
    rewards = table[:, 1:2] + table[:, 2:3] + table[:, 3:4]
    same = jnp.where(ids == prompt_ref[...].astype(F32), 1.0, 0.0)
    count = jnp.maximum(jnp.sum(same, axis=0, keepdims=True), 1.0)
    mean = jnp.sum(same * rewards, axis=0, keepdims=True) / count
    square = jnp.sum(same * (rewards * rewards), axis=0, keepdims=True) / count
    spread_1 = jnp.sqrt(jnp.maximum(square - mean * mean, 1.0))
    advantage = (reward_ref[...] - mean) / spread_1

    grad = (GA[0:FEAT, :] + GA[FEAT : 2 * FEAT, :]) * (advantage * (-1.0 / 16.0))
    GS[...] = jnp.zeros_like(GS)
    for j in range(5):
        GS[:, j, :] = grad[:, 128 * j : 128 * (j + 1)]

    def column_copy(k):
        peer = lax.rem(dev + k, 16)
        return to_peer(GS.at[peer], GR.at[dev], r_send.at[k], r_recv.at[k], (sec, peer))

    for k in range(1, 16):
        column_copy(k).start()
    GR[dev] = GS[dev]
    for k in range(1, 16):
        column_copy(k).wait()
    R1[...] = jnp.sum(GR[...], axis=0)

    def row_copy(k):
        return to_peer(R1, RR.at[sec], s_send.at[k], s_recv.at[k], (lax.rem(sec + k, 16), dev))

    for k in range(1, 16):
        row_copy(k).start()
    RR[sec] = R1[...]
    for k in range(1, 16):
        row_copy(k).wait()
    total = jnp.sum(RR[...], axis=0)
    picked = jnp.zeros((SHARD, 128), F32)
    want = iota((SHARD, 128), 0) + sec * SHARD
    for j in range(5):
        picked = jnp.where(iota((SHARD, 128), 1) + 128 * j == want, jnp.broadcast_to(total[j : j + 1], (SHARD, 128)), picked)
    g = jnp.sum(picked, axis=1, keepdims=True)
    m1 = 0.9 * m1_ref[...] + 0.1 * g
    m2 = 0.999 * m2_ref[...] + 0.001 * g * g
    m1_out[...] = m1
    m2_out[...] = m2
    w_new_out[...] = w_final_ref[...] - learn_rate * m1 / (jnp.sqrt(m2) + 1e-08)


def to_features(latent):
    lead = latent.shape[0]
    blocks = latent.reshape(lead, 4, ROWS, 2, COLS, 2)
    return blocks.transpose(0, 1, 3, 5, 2, 4).reshape(lead, FEAT, TOK)


def per_device(
    latents,
    noise,
    rewards,
    prompt_ids,
    context,
    time_bias,
    gain_first,
    gain_second,
    gain_third,
    w_in,
    w_conv,
    w_query,
    w_key,
    w_value,
    w_attn_out,
    w_final,
    moment_first,
    moment_second,
):
    lat = to_features(latents)[0]
    noi = to_features(noise.reshape(STEPS, 4, 2 * ROWS, 2 * COLS))
    own = lax.dynamic_index_in_dim(context, prompt_ids[0], 0, keepdims=False)
    own = jnp.pad(own, ((0, 3), (0, 0)))
    vmem = pl.BlockSpec(memory_space=pltpu.VMEM)
    small = jax.ShapeDtypeStruct((SHARD, 1), F32)
    dma = pltpu.SemaphoreType.DMA
    x_new, w_new, m1, m2 = pl.pallas_call(
        body,
        out_shape=(jax.ShapeDtypeStruct((FEAT, TOK), F32), small, small, small),
        in_specs=[vmem] * 18,
        out_specs=(vmem,) * 4,
        scratch_shapes=[
            pltpu.VMEM((NZ, 2, NX, 2, 2, SHARD, LANES), BF16),
            pltpu.VMEM((16, 88, 128), BF16),
            pltpu.VMEM((16, 80, 128), BF16),
            pltpu.VMEM((LANES, SHARD), F32),
            pltpu.VMEM((9 * C, C), BF16),
            pltpu.VMEM((C, C), BF16),
            pltpu.VMEM((C, C), BF16),
            pltpu.VMEM((128, C), F32),
            pltpu.VMEM((NZ, 2, SHARD, 128), F32),
            pltpu.VMEM((PAIRS, 128, 256), BF16),
            pltpu.VMEM((PAIRS, 256, 128), BF16),
            pltpu.VMEM((STEPS + 1, TOK + 2 * COLS, 128), BF16),
            pltpu.VMEM((TOK + 2 * COLS, 3 * C), BF16),
            pltpu.VMEM((TOK, C), F32),
            pltpu.VMEM((TOK, C), F32),
            pltpu.VMEM((TOK, 128), F32),
            pltpu.VMEM((STEPS, TOK, 128), F32),
            pltpu.VMEM((STEPS, 2 * FEAT, TOK), BF16),
            pltpu.VMEM((TOK, C), BF16),
            pltpu.VMEM((2 * FEAT, C), F32),
            pltpu.VMEM((16, 8, 128), F32),
            pltpu.VMEM((16, 8, 128), F32),
            pltpu.VMEM((8, 128), F32),
            pltpu.VMEM((16, 8, 128), F32),
            dma((3, 3, 2, 4)),
            dma((3, 3, 2, 4)),
            dma((16,)),
            dma((16,)),
            dma((16,)),
            dma((16,)),
            dma((16,)),
            dma((16,)),
            dma((STEPS, 2)),
            dma((STEPS, 2)),
            dma((16,)),
            dma((16,)),
            dma((16,)),
            dma((16,)),
        ],
        compiler_params=pltpu.CompilerParams(
            collective_id=0, has_side_effects=True, vmem_limit_bytes=58 * 1024 * 1024
        ),
        name="ddpo",
    )(
        lat,
        noi,
        rewards.reshape(1, 1),
        prompt_ids.reshape(1, 1),
        own,
        time_bias,
        gain_first.reshape(1, C),
        gain_second.reshape(1, C),
        gain_third.reshape(1, C),
        w_in,
        w_conv,
        w_query,
        w_key,
        w_value,
        w_attn_out,
        w_final,
        moment_first,
        moment_second,
    )
    blocks = x_new.reshape(4, 2, 2, ROWS, COLS)
    latent = blocks.transpose(0, 3, 1, 4, 2).reshape(1, 4, 2 * ROWS, 2 * COLS)
    return (latent, w_new, m1, m2)


def solution(mesh):
    placed = (
        P("sec", None, "dev", None),
        P(None, "sec", None, "dev", None),
        P("sec"),
        P("sec"),
        P(),
        P(),
        P(),
        P(),
        P(),
        P("sec", "dev"),
        P("sec", "dev"),
        P("sec", "dev"),
        P("sec", "dev"),
        P("sec", "dev"),
        P("sec", "dev"),
        P("sec", "dev"),
        P("sec", "dev"),
        P("sec", "dev"),
    )
    return jax.shard_map(
        per_device,
        mesh=mesh,
        in_specs=placed,
        out_specs=(P("sec", None, "dev", None), P("sec", "dev"), P("sec", "dev"), P("sec", "dev")),
        check_vma=False,
    )
```

time: 614 us -> 149 us (0.24)
  blocking collectives: 434 us -> 0 us
  Pallas kernels: 0 us -> 125 us
  matrix products: 60.3 us -> 0 us
  starting transfers between devices: 28.7 us -> 0 us
  waiting for transfers between devices: 18.2 us -> 0 us
  between operations: 19 us -> 2.05 us
  local copies, waits for them, and re-layouts: 36 us -> 22.1 us
  other arithmetic: 12.7 us -> 0 us
    all_gather x10 -> x0, blocking collectives: 309 us -> none  [the longest x1 51.1 us: per_device(): lax.all_gather(in_rows, 'dev', axis=1, tiled=True)]
    pallas_call x0 -> x1, Pallas kernels: none -> 125 us  [per_device(): pl.pallas_call(body, out_shape=(jax.ShapeDtypeStruct((FEAT, TOK), F32), s...]
    unnamed x2 -> x0, blocking collectives: 99.3 us -> none
    dot_general x51 -> x0, matrix products: 60.3 us -> none  [the longest x6 32.1 us: denoise(): jnp.dot(columns.reshape(flat_rows, 9 * channels), w_conv, preferred_eleme...]
    ppermute x12 -> x0, starting transfers between devices: 28.5 us -> none  [the longest x6 15.2 us: padded_2(): after = lax.ppermute(first, axis, down)]
    psum x1 -> x0, blocking collectives: 25.5 us -> none  [per_device(): lax.psum((jnp.sum(onehot, axis=0), jnp.sum(onehot * rewards[:, None], axi...]
    ppermute x12 -> x0, waiting for transfers between devices: 18.2 us -> none  [the longest x6 18.1 us: padded_2(): after = lax.ppermute(first, axis, down)]
    mul x36 -> x0, local copies, waits for them, and re-layouts: 11.3 us -> none  [the longest x18 7.57 us: per_device(): weighted = noise_patch * (advantage[:, None, None] * (beta / sigma))]
  transfers between devices with their start and end apart: 15 -> 0, of which waited for: 5 -> 0; matrix products, arithmetic and copies ran while one was open for 7% -> 0% of each run, Pallas kernels for 0% -> 0%
where the time goes in v1:
time: 149 us
  Pallas kernels  125 us (84%)
  local copies, waits for them, and re-layouts  22.1 us (15%)
  between operations  2.05 us (1%)
    pallas_call x1, Pallas kernels, per_device(): pl.pallas_call(body, out_shape=(jax.ShapeDtypeStruct((FEAT, TOK), F32), s...  125 us
    unnamed x33, local copies, waits for them, and re-layouts  13.2 us
    transpose x2, local copies, waits for them, and re-layouts, to_features(): return blocks.transpose(0, 1, 3, 5, 2, 4).reshape(lead, FEAT, TOK)  3.08 us

profile of v1, /device:TPU:1, one launch (start us, length us, event | category | flops | bytes accessed | tf_op | source)
XLA Modules:
  0.0 148.9 jit_solution(4726130638222329142)
XLA Ops:
  0.6 1.1 copy.34
  1.7 0.2 copy.35
  2.0 0.7 squeeze_reshape.3.lat_ref
  2.7 2.9 %copy.36 = f32[6,1,4,8,128]{0,4,3,2,1:T(8,128)} copy(f32[6,1,4,8,128]{4,3,2,1,0:T(8,128)} %param.19) | data formatting | bytes 196608 | tf_op args[1]
  5.6 2.9 %copy.37 = f32[6,4,2,2,4,64]{5,4,3,2,1,0:T(4,128)S(1)} copy(f32[6,4,2,2,4,64]{0,3,5,2,4,1:T(2,128)} %bitcast.20) | data formatting | bytes 196608 | tf_op jit(solution)/shard_map/transpose | solution.py:500
  8.5 0.8 reshape.36.noise_ref
  10.6 0.7 constant_dynamic-slice_fusion
  11.5 0.8 pad.4.ctx_ref
  12.2 0.6 reshape.39.g1_ref
  12.8 0.6 reshape.40.g2_ref
  13.4 0.6 reshape.41.g3_ref
  14.0 0.7 copy.39.w_conv_ref
  14.8 0.7 copy.40.w_key_ref
  15.5 0.7 copy.41.w_value_ref
  16.2 0.7 copy.42.w_final_ref
  16.9 0.7 copy.43.m1_ref
  17.6 0.7 copy.44.m2_ref
  18.3 124.8 %ddpo.1 = (f32[16,256]{1,0:T(8,128)}, f32[40,1]{1,0:T(8,128)}, f32[40,1]{1,0:T(8,128)}, f32[40,1]{1,0:T(8,128)}) custom-call(f32[16,256]{1,0:T(8,128)} %squeeze_reshape.3.lat_ref, f32[6,16,256]{2,1,0:T(8,128)} %reshape.36.noise_ref, f32[1,1]{1,0:T(1,128)} %bitcast.15.reward_ref, s32[1,1]{1,0:T(1,128)} %bitcast.16.prompt_ref, bf16[80,2048]{1,0:T(8,128)(2,1)} %pad.4.ctx_ref, ...), custom_call_target="tpu_custom_call" | custom-call | tf_op jit(solution)/shard_map/ddpo/pallas_call | solution.py:530
  143.1 0.8 reshape.42
  143.9 0.3 copy.45
  144.2 0.8 copy.46
  144.9 1.3 copy.47
  146.3 1.3 copy.48
  147.6 1.3 copy.49
  (21 shorter events, 0.2 us)
Async XLA Ops:
  0.6 10.0 %copy-start = (bf16[8,77,2048]{2,0,1:T(8,128)(2,1)S(1)}, bf16[8,77,2048]{2,0,1:T(8,128)(2,1)}, u32[]{:S(2)}) copy-start(bf16[8,77,2048]{2,0,1:T(8,128)(2,1)} %param.22) | copy-start | bytes 7569412
  5.5 6.7 %copy-start.4 = (f32[640]{0:T(1024)S(1)}, f32[640]{0:T(1024)}, u32[]{:S(2)}) copy-start(f32[640]{0:T(1024)} %param.24) | copy-start | bytes 7684
  5.6 7.3 %copy-start.5 = (f32[640]{0:T(1024)S(1)}, f32[640]{0:T(1024)}, u32[]{:S(2)}) copy-start(f32[640]{0:T(1024)} %param.25) | copy-start | bytes 7684
  5.6 7.9 %copy-start.6 = (f32[640]{0:T(1024)S(1)}, f32[640]{0:T(1024)}, u32[]{:S(2)}) copy-start(f32[640]{0:T(1024)} %param.26) | copy-start | bytes 7684
  5.6 8.5 %copy-start.1 = (bf16[360,40]{0,1:T(8,128)(2,1)S(1)}, bf16[360,40]{0,1:T(8,128)(2,1)}, u32[]{:S(2)}) copy-start(bf16[360,40]{0,1:T(8,128)(2,1)} %param.28) | copy-start | bytes 86404
  5.6 9.2 %copy-start.2 = (bf16[128,40]{0,1:T(8,128)(2,1)S(1)}, bf16[128,40]{0,1:T(8,128)(2,1)}, u32[]{:S(2)}) copy-start(bf16[128,40]{0,1:T(8,128)(2,1)} %param.30) | copy-start | bytes 30724
  5.6 9.9 %copy-start.3 = (bf16[128,40]{0,1:T(8,128)(2,1)S(1)}, bf16[128,40]{0,1:T(8,128)(2,1)}, u32[]{:S(2)}) copy-start(bf16[128,40]{0,1:T(8,128)(2,1)} %param.31) | copy-start | bytes 30724
  5.6 10.6 %copy-start.7 = (f32[40,1]{0,1:T(1,128)S(1)}, f32[40,1]{0,1:T(1,128)}, u32[]{:S(2)}) copy-start(f32[40,1]{0,1:T(1,128)} %param.33) | copy-start | bytes 484
  5.6 11.3 %copy-start.8 = (f32[40,1]{0,1:T(1,128)S(1)}, f32[40,1]{0,1:T(1,128)}, u32[]{:S(2)}) copy-start(f32[40,1]{0,1:T(1,128)} %param.34) | copy-start | bytes 484
  5.6 12.0 %copy-start.9 = (f32[40,1]{0,1:T(1,128)S(1)}, f32[40,1]{0,1:T(1,128)}, u32[]{:S(2)}) copy-start(f32[40,1]{0,1:T(1,128)} %param.35) | copy-start | bytes 484

commit v2 on v1

v2 whole, which is shorter than its diff:
```python
import math

import jax
import jax.numpy as jnp
from jax import lax
from jax.experimental import pallas as pl
from jax.experimental.pallas import tpu as pltpu
from jax.sharding import PartitionSpec as P

HEAD = 64
STEPS = 6
ROWS = 4
COLS = 64
TOK = ROWS * COLS
C = 640
FEAT = 16
PAIRS = C // (2 * HEAD)
SHARD = 40
CONV_ROWS = 360
LANES = 512
FINAL_AT = 384
QUERY_AT = 400
OUT_AT = 440
IN_AT = 480
CTX_TOK = 77

alpha_bars = (0.1, 0.15, 0.21, 0.28, 0.36, 0.45, 0.55)
norm_eps = 1e-06
learn_rate = 0.001
NX, NY, NZ = 4, 4, 8
SIZE = {"x": NX, "y": NY, "z": NZ}
CLASSES = (
    ((0, 16), "zyx"),
    ((16, 32), "zxy"),
    ((32, 40), "xyz"),
)
MESH_ID = pl.DeviceIdType.MESH
F32 = jnp.float32
BF16 = jnp.bfloat16


def plan(step_index):
    current = alpha_bars[step_index]
    following = alpha_bars[step_index + 1]
    sigma = math.sqrt((1.0 - following) / (1.0 - current)) * math.sqrt(1.0 - current / following)
    scale = math.sqrt(following / current)
    beta = math.sqrt(1.0 - following - sigma * sigma) - scale * math.sqrt(1.0 - current)
    return (scale, beta, sigma)


PLANS = [plan(i) for i in range(STEPS)]


def dot(a, b):
    return jnp.dot(a, b, preferred_element_type=F32)


def dot_t(a, b):
    return lax.dot_general(a, b, (((1,), (1,)), ((), ())), preferred_element_type=F32)


def rms(values, gain):
    mean_square = jnp.mean(values * values, axis=-1, keepdims=True)
    return values * lax.rsqrt(mean_square + norm_eps) * gain


def silu(v):
    half = 0.5 * v
    return half + half * jnp.tanh(half)


def choose(index, values):
    out = jnp.float32(values[0])
    for i in range(1, len(values)):
        out = jnp.where(index == i, jnp.float32(values[i]), out)
    return out


def iota(shape, dim):
    return lax.broadcasted_iota(jnp.int32, shape, dim)


def body(
    lat_ref,
    noise_ref,
    reward_ref,
    prompt_ref,
    ctx_ref,
    bias_ref,
    g1_ref,
    g2_ref,
    g3_ref,
    w_in_ref,
    w_conv_ref,
    w_query_ref,
    w_key_ref,
    w_value_ref,
    w_out_ref,
    w_final_ref,
    x_out,
    g_out,
    CX,
    G,
    KG,
    KT,
    Wc,
    Wq,
    Wo,
    Win,
    WS,
    WF,
    WI,
    Kbd,
    Vbd,
    PB,
    A,
    H,
    M,
    X,
    NZT,
    NTS,
    FA,
    GA,
    GS,
    GR,
    R1,
    RR,
    a_send,
    a_recv,
    l_send,
    l_recv,
    g_send,
    g_recv,
    b_send,
    b_recv,
    k_send,
    k_recv,
    t_send,
    t_recv,
    h_send,
    h_recv,
    r_send,
    r_recv,
    s_send,
    s_recv,
    c_sem,
):
    sec = lax.axis_index("sec")
    dev = lax.axis_index("dev")
    z, ylo = sec // 2, sec % 2
    xx, yhi, core = dev // 4, (dev // 2) % 2, dev % 2
    yy = yhi * 2 + ylo
    me = {"x": xx, "y": yy, "z": z}

    def device(x, y, zc, c):
        return (zc * 2 + y % 2, x * 4 + (y // 2) * 2 + c)

    def neighbour(axis, delta):
        pos = dict(me)
        pos[axis] = lax.rem(me[axis] + delta + SIZE[axis], SIZE[axis])
        return device(pos["x"], pos["y"], pos["z"], core)

    barrier = pltpu.get_barrier_semaphore()
    cross_y = (sec - 2 * ylo + 1, dev - 2 * yhi + 2 * (1 - yhi))
    for k in range(1, 16):
        pl.semaphore_signal(barrier, inc=1, device_id=(lax.rem(sec + k, 16), dev), device_id_type=MESH_ID)
        pl.semaphore_signal(barrier, inc=1, device_id=(sec, lax.rem(dev + k, 16)), device_id_type=MESH_ID)
    pl.semaphore_signal(barrier, inc=1, device_id=cross_y, device_id_type=MESH_ID)

    context_copy = pltpu.make_async_copy(ctx_ref, CX, c_sem)
    context_copy.start()

    eye = (iota((SHARD, SHARD), 0) == iota((SHARD, SHARD), 1)).astype(BF16)
    lane40 = iota((SHARD, 128), 1)
    row40 = iota((SHARD, 128), 0)

    def place(square, at):
        turned = dot_t(eye, square).astype(BF16)
        return dot(turned, (lane40 == row40 + (at - FINAL_AT)).astype(BF16))

    def stand(row):
        wide = jnp.broadcast_to(row.astype(F32), (SHARD, SHARD))
        on_diagonal = iota((SHARD, SHARD), 0) == iota((SHARD, SHARD), 1)
        return jnp.sum(jnp.where(on_diagonal, wide, 0.0), axis=1, keepdims=True)

    tail = place(w_query_ref[...], QUERY_AT) + place(w_out_ref[...], OUT_AT)
    tail = jnp.where(lane40 == IN_AT - FINAL_AT, stand(w_in_ref[...]), tail)
    tail = jnp.where(lane40 == dev, stand(w_final_ref[...]), tail)
    G[z, ylo, xx, yhi, core, :, 256:FINAL_AT] = jnp.zeros((SHARD, 128), BF16)
    G[z, ylo, xx, yhi, core, :, 0:CONV_ROWS] = w_conv_ref[...]
    G[z, ylo, xx, yhi, core, :, FINAL_AT:LANES] = tail.astype(BF16)

    pick = iota((128, 128), 1) == 2 * (iota((128, 128), 0) % COLS) + iota((128, 128), 0) // COLS
    pick = pick.astype(BF16)

    def split(v):
        top = v.astype(BF16)
        rest = v - top.astype(F32)
        mid = rest.astype(BF16)
        return top, mid, (rest - mid.astype(F32)).astype(BF16)

    own_row = iota((TOK, 2 * 32), 0) // COLS == (iota((TOK, 2 * 32), 1) % 8) // 2

    def turn(rows32):
        cols = sum(dot_t(pick, part) for part in split(rows32))
        both = jnp.concatenate([cols[0:COLS], cols[COLS : 2 * COLS]], axis=1)
        return jnp.where(own_row, jnp.concatenate([both] * ROWS, axis=0), 0.0)

    pl.semaphore_wait(barrier, 31)

    def halo_copy(t, up):
        if up:
            src, dst, to, i = PB.at[t, pl.ds(COLS, COLS)], PB.at[t, pl.ds(COLS + TOK, COLS)], dev - 1, 0
        else:
            src, dst, to, i = PB.at[t, pl.ds(TOK, COLS)], PB.at[t, pl.ds(0, COLS)], dev + 1, 1
        return pltpu.make_async_remote_copy(
            src, dst, h_send.at[t, i], h_recv.at[t, i], device_id=(sec, to), device_id_type=MESH_ID
        )

    def start_halo(t):
        @pl.when(dev > 0)
        def _():
            halo_copy(t, True).start()

        @pl.when(dev < 15)
        def _():
            halo_copy(t, False).start()

    def wait_halo(t):
        @pl.when(dev > 0)
        def _():
            halo_copy(t, True).wait_send()
            halo_copy(t, False).wait_recv()

        @pl.when(dev < 15)
        def _():
            halo_copy(t, False).wait_send()
            halo_copy(t, True).wait_recv()

    def to_peer(src, dst, send, recv, peer):
        return pltpu.make_async_remote_copy(src, dst, send, recv, device_id=peer, device_id_type=MESH_ID)

    def key_copy(k):
        return to_peer(KG.at[sec], KG.at[sec], k_send.at[k], k_recv.at[k], (lax.rem(sec + k, 16), dev))

    sent = []
    pushes = []

    def region(rows, half, **where):
        zi, xi = where["z"], where["x"]
        zi = pl.ds(0, NZ) if zi is None else zi
        xi = pl.ds(0, NX) if xi is None else xi
        if where["y"] is None:
            lo_i, hi_i = pl.ds(0, 2), pl.ds(0, 2)
        else:
            lo_i, hi_i = where["y"] % 2, where["y"] // 2
        lanes = pl.ds(0, LANES) if half is None else pl.ds(half * (LANES // 2), LANES // 2)
        return G.at[zi, lo_i, xi, hi_i, core, pl.ds(rows[0], rows[1] - rows[0]), lanes]

    def along(axis, delta):
        return lax.rem(me[axis] + delta + SIZE[axis], SIZE[axis])

    def gather(k, rows, order):
        first, second, third = order
        n = SIZE[third]

        def block_copy(j):
            ref = region(rows, None, **me)
            return to_peer(ref, ref, a_send.at[k, j], a_recv.at[k, j], neighbour(first, j))

        def line_copy(j):
            ref = region(rows, None, **{first: None, second: me[second], third: me[third]})
            return to_peer(ref, ref, l_send.at[k, j], l_recv.at[k, j], neighbour(second, j))

        def ring_copy(j, direction, r):
            step = 1 if direction == 0 else -1
            half = direction if r == n // 2 else None
            place_ = {first: None, second: along(second, -j), third: along(third, -step * (r - 1))}
            ref = region(rows, half, **place_)
            return to_peer(
                ref, ref, g_send.at[k, j, direction, r - 1], g_recv.at[k, j, direction, r - 1], neighbour(third, step)
            )

        def push(j, delta):
            place_ = {first: None, second: None if j is None else along(second, -j), third: along(third, delta)}
            ref = region(rows, None, **place_)
            i = len(pushes)
            c = to_peer(ref, ref, b_send.at[i], b_recv.at[i], (sec, dev + 1 - 2 * core))
            c.start()
            pushes.append(c)

        def start(c):
            c.start()
            sent.append(c)

        for j in range(1, SIZE[first]):
            start(block_copy(j))
        yield
        for j in range(1, SIZE[first]):
            block_copy(j).wait_recv()
        for j in (1, 3, 2):
            start(line_copy(j))
        for direction in (0, 1):
            start(ring_copy(0, direction, 1))
        yield
        for j in (1, 3, 2):
            line_copy(j).wait_recv()
            for direction in (0, 1):
                start(ring_copy(j, direction, 1))
            yield
        push(None, 0)
        for r in range(2, n // 2 + 1):
            for j in (0, 1, 3, 2):
                for direction in (0, 1):
                    ring_copy(j, direction, r - 1).wait_recv()
                    start(ring_copy(j, direction, r))
                yield
            push(None, r - 1)
            push(None, -(r - 1))
        for j in (0, 1, 3, 2):
            for direction in (0, 1):
                ring_copy(j, direction, n // 2).wait_recv()
            push(j, n // 2)
            yield

    def keys_and_values():
        KG[sec, 0:SHARD, :] = w_key_ref[...]
        KG[sec, SHARD : 2 * SHARD, :] = w_value_ref[...]
        reward = jnp.broadcast_to(reward_ref[...], (8, 128))
        prompt = jnp.broadcast_to(prompt_ref[...].astype(F32), (8, 128))
        hi = reward.astype(BF16).astype(F32)
        mid = (reward - hi).astype(BF16).astype(F32)
        low = reward - hi - mid
        lane8 = iota((8, 128), 1)
        stats = jnp.where(lane8 == 0, prompt, 0.0)
        for i, part in enumerate((hi, mid, low)):
            stats = jnp.where(lane8 == i + 1, part, stats)
        KG[sec, 80:88, :] = stats.astype(BF16)
        yield
        yield
        for k in range(1, 16):
            key_copy(k).start()
        yield
        yield
        yield
        yield
        yield
        yield
        for k in range(1, 16):
            key_copy(k).wait()
        wide = jnp.concatenate([KG[s, 0:80, :] for s in range(16)], axis=1)
        context_copy.wait()
        every = dot_t(wide, CX[...]).astype(BF16)
        n = CX.shape[0]
        mine = iota((n, 128), 0) == 8 * iota((n, 128), 1) + prompt_ref[...]
        KT[dev] = dot(every, mine.astype(BF16)).astype(BF16)

        def copy(k):
            return to_peer(KT.at[dev], KT.at[dev], t_send.at[k], t_recv.at[k], (sec, lax.rem(dev + k, 16)))

        for k in range(1, 16):
            copy(k).start()
        yield
        yield
        yield
        yield
        yield
        yield
        for k in range(1, 16):
            copy(k).wait()
        kt = jnp.concatenate([KT[d, 0:SHARD, :] for d in range(16)], axis=0)
        vt = jnp.concatenate([KT[d, SHARD : 2 * SHARD, :] for d in range(16)], axis=0)
        v = jnp.transpose(vt.astype(F32))
        row = iota((128, 128), 0)
        lane = iota((128, 128), 1)
        for p in range(PAIRS):
            part = kt[128 * p : 128 * (p + 1), :].astype(F32) * (1.0 / math.sqrt(HEAD))
            Kbd[p, :, 0:128] = jnp.where(row < HEAD, part, 0.0).astype(BF16)
            Kbd[p, :, 128:256] = jnp.where(row < HEAD, 0.0, part).astype(BF16)
            part = v[:, 128 * p : 128 * (p + 1)]
            Vbd[p, 0:128, :] = jnp.where(lane < HEAD, part, 0.0).astype(BF16)
            Vbd[p, 128:256, :] = jnp.where(lane < HEAD, 0.0, part).astype(BF16)

    def tokens():
        X[...] = jnp.zeros_like(X)
        X[:, 0:64] = turn(lat_ref[...])
        PB[0, COLS : COLS + TOK, :] = X[...].astype(BF16)
        start_halo(0)
        yield
        yield
        GA[...] = jnp.zeros_like(GA)
        GS[...] = jnp.zeros_like(GS)
        Win[...] = jnp.zeros_like(Win)
        for t in range(STEPS):
            yield
            yield
            nt = turn(noise_ref[32 * t : 32 * (t + 1), :])
            NZT[t] = jnp.concatenate([nt, jnp.zeros_like(nt)], axis=1)
            top = nt.astype(BF16).astype(F32)
            NTS[t] = jnp.transpose(jnp.concatenate([top, nt - top], axis=1)).astype(BF16)

    running = [gather(k, rows, order) for k, (rows, order) in enumerate(CLASSES)]
    running += [keys_and_values(), tokens()]
    while running:
        left = []
        for g in running:
            try:
                next(g)
                left.append(g)
            except StopIteration:
                pass
        running = left
    for c in sent:
        c.wait_send()
    for c in pushes:
        c.wait()

    lane_w = iota((SHARD, 128), 1)

    def settle(zi, carry):
        turned = []
        for lo in range(2):
            parts = G[zi, lo].astype(F32)
            flat = parts.reshape(C, LANES)
            tail = jnp.sum(parts.reshape(16, SHARD, LANES)[:, :, FINAL_AT:LANES], axis=0)
            WS[zi, lo] = jnp.where(lane_w < FEAT, tail, 0.0)
            turned.append(jnp.transpose(flat))
        conv = jnp.concatenate([w[0:CONV_ROWS] for w in turned], axis=0).astype(BF16)
        Wc[pl.ds(pl.multiple_of(zi * 2 * CONV_ROWS, 16), 2 * CONV_ROWS), :] = conv
        at = pl.ds(pl.multiple_of(zi * 2 * SHARD, 16), 2 * SHARD)
        Wq[at, :] = jnp.concatenate([w[QUERY_AT : QUERY_AT + SHARD] for w in turned], axis=0).astype(BF16)
        Wo[at, :] = jnp.concatenate([w[OUT_AT : OUT_AT + SHARD] for w in turned], axis=0).astype(BF16)
        for lo in range(2):
            Win[pl.ds(zi * 2 + lo, 1), :] = turned[lo][IN_AT : IN_AT + 1]
        return carry

    lax.fori_loop(0, NZ, settle, 0)

    def spread_of(lane, feature):
        return (lane < 64) & (feature == ((lane // 8) % 4) * 4 + (lane % 2) * 2 + lane // 32)

    by_col = spread_of(iota((128, 128), 1), iota((128, 128), 0)).astype(BF16)
    by_row = spread_of(iota((128, 128), 0), iota((128, 128), 1)).astype(BF16)
    WF[...] = dot(WS[...].reshape(C, 128).astype(BF16), by_col).astype(BF16)
    WI[...] = dot(by_row, Win[...].astype(BF16)).astype(BF16)
    valid = iota((TOK, 128), 0) // COLS == (iota((TOK, 128), 1) % 8) // 2

    token_col = iota((TOK, C), 0) % COLS
    tok_row = iota((2 * HEAD * 2, 2 * HEAD * 2), 0)
    tok_col = iota((2 * HEAD * 2, 2 * HEAD * 2), 1)
    ones = (((tok_row < 128) == (tok_col < 128)) & (tok_row % 128 < CTX_TOK)).astype(BF16)

    def spread(act, at, n):
        col = iota((n, C), 0) % COLS
        rows = pl.ds(at, n)
        A[rows, C : 2 * C] = act.astype(BF16)
        A[rows, 0:C] = jnp.where(col == 0, 0.0, pltpu.roll(act, 1, 0)).astype(BF16)
        A[rows, 2 * C : 3 * C] = jnp.where(col == COLS - 1, 0.0, pltpu.roll(act, n - 1, 0)).astype(BF16)

    def denoise(t, carry):
        scale = choose(t, [p[0] for p in PLANS])
        beta = choose(t, [p[1] for p in PLANS])
        sigma = choose(t, [p[2] for p in PLANS])
        weight = choose(t, [p[1] / p[2] for p in PLANS])
        bias = bias_ref[pl.ds(t, 1), :]
        w_first = WI[...]
        hidden = dot(PB[t, COLS : COLS + TOK, :], w_first) + bias
        H[...] = hidden
        spread(silu(rms(hidden, g1_ref[...].reshape(1, C))), COLS, TOK)
        M[...] = H[...] + dot(A[COLS : COLS + TOK, :], Wc[3 * C : 6 * C, :])
        wait_halo(t)
        edge = jnp.concatenate([PB[t, 0:COLS, :], PB[t, COLS + TOK :, :]], axis=0)
        act = silu(rms(dot(edge, w_first) + bias, g1_ref[...].reshape(1, C)))
        above = jnp.where(dev > 0, act[0:COLS], 0.0)
        below = jnp.where(dev < 15, act[COLS:], 0.0)
        spread(above, 0, COLS)
        spread(below, COLS + TOK, COLS)
        M[...] += dot(A[0:TOK, :], Wc[0 : 3 * C, :])
        M[...] += dot(A[2 * COLS : 2 * COLS + TOK, :], Wc[6 * C : 9 * C, :])

        def finish(ranges):
            def load(ref, *lead):
                return jnp.concatenate([ref[(*lead, slice(a, b))] for a, b in ranges], axis=0)

            mixed = load(M)
            normed = rms(mixed, g2_ref[...].reshape(1, C)).astype(BF16)
            queries = dot(normed, Wq[...]).astype(BF16)
            heads = []
            for p in range(PAIRS):
                e = jnp.exp(dot(queries[:, 128 * p : 128 * (p + 1)], Kbd[p]))
                total = dot(e.astype(BF16), ones)
                heads.append(dot((e * (1.0 / total)).astype(BF16), Vbd[p]).astype(BF16))
            out = mixed + dot(jnp.concatenate(heads, axis=1), Wo[...])
            final = silu(rms(out, g3_ref[...].reshape(1, C))).astype(BF16)
            keep = jnp.concatenate([valid[a:b] for a, b in ranges], axis=0)
            predicted = jnp.where(keep, dot(final, WF[...]), 0.0)
            x_new = scale * load(X) + beta * predicted + sigma * load(NZT, t)
            at = 0
            for a, b in ranges:
                n = b - a
                FA[a:b, :] = final[at : at + n]
                X[a:b, :] = x_new[at : at + n]
                PB[t + 1, a + COLS : b + COLS, :] = x_new[at : at + n].astype(BF16)
                at += n

        finish(((0, TOK),))

        @pl.when(t < STEPS - 1)
        def _():
            start_halo(t + 1)

        GA[...] += weight * dot(NTS[t], FA[...])
        return carry

    table = jnp.concatenate([KG[s, 80:88, :].astype(F32)[0:1] for s in range(16)], axis=0)
    ids = table[:, 0:1]
    rewards = table[:, 1:2] + table[:, 2:3] + table[:, 3:4]
    same = jnp.where(ids == prompt_ref[...].astype(F32), 1.0, 0.0)
    count = jnp.maximum(jnp.sum(same, axis=0, keepdims=True), 1.0)
    mean = jnp.sum(same * rewards, axis=0, keepdims=True) / count
    square = jnp.sum(same * (rewards * rewards), axis=0, keepdims=True) / count
    spread_1 = jnp.sqrt(jnp.maximum(square - mean * mean, 1.0))
    advantage = (reward_ref[...] - mean) / spread_1

    lax.fori_loop(0, STEPS, denoise, 0)

    lane128 = iota((FEAT, 128), 1)
    fold = spread_of(lane128 % 64, iota((FEAT, 128), 0)).astype(BF16)
    grad = sum(dot(fold, part) for part in split(GA[...])) * (advantage * (-1.0 / 16.0))
    for j in range(5):
        GS[:, j, :] = grad[:, 128 * j : 128 * (j + 1)]

    def column_copy(k):
        peer = lax.rem(dev + k, 16)
        return to_peer(GS.at[peer], GR.at[dev], r_send.at[k], r_recv.at[k], (sec, peer))

    for k in range(1, 16):
        column_copy(k).start()
    GR[dev] = GS[dev]
    flat = X[0:COLS, 0:64]
    for r in range(1, ROWS):
        flat = flat + X[r * COLS : (r + 1) * COLS, 0:64]
    flat = jnp.concatenate([flat[:, 0:32], flat[:, 32:64]], axis=0)
    x_out[...] = sum(
        lax.dot_general(part, pick, (((0,), (0,)), ((), ())), preferred_element_type=F32) for part in split(flat)
    )
    for k in range(1, 16):
        column_copy(k).wait()
    R1[...] = jnp.sum(GR[...], axis=0)

    def row_copy(k):
        return to_peer(R1, RR.at[sec], s_send.at[k], s_recv.at[k], (lax.rem(sec + k, 16), dev))

    for k in range(1, 16):
        row_copy(k).start()
    RR[sec] = R1[...]
    for k in range(1, 16):
        row_copy(k).wait()
    total = jnp.sum(RR[...], axis=0)
    picked = jnp.zeros((128, 128), F32)
    want = iota((128, 128), 0) + sec * SHARD
    for j in range(5):
        hit = iota((128, 128), 1) + 128 * j == want
        picked = jnp.where(hit, jnp.broadcast_to(total[j : j + 1], (128, 128)), picked)
    g_out[...] = jnp.sum(jnp.transpose(picked), axis=0, keepdims=True)[:, 0:SHARD]


def per_device(
    latents,
    noise,
    rewards,
    prompt_ids,
    context,
    time_bias,
    gain_first,
    gain_second,
    gain_third,
    w_in,
    w_conv,
    w_query,
    w_key,
    w_value,
    w_attn_out,
    w_final,
    moment_first,
    moment_second,
):
    words, width = context.shape[1:]
    flat_context = context.transpose(1, 0, 2).reshape(words * context.shape[0], width)
    vmem = pl.BlockSpec(memory_space=pltpu.VMEM)
    dma = pltpu.SemaphoreType.DMA
    x_new, grad = pl.pallas_call(
        body,
        out_shape=(jax.ShapeDtypeStruct((32, 128), F32), jax.ShapeDtypeStruct((1, SHARD), F32)),
        in_specs=[vmem] * 4 + [pl.BlockSpec(memory_space=pl.ANY)] + [vmem] * 11,
        out_specs=(vmem,) * 2,
        scratch_shapes=[
            pltpu.VMEM(flat_context.shape, BF16),
            pltpu.VMEM((NZ, 2, NX, 2, 2, SHARD, LANES), BF16),
            pltpu.VMEM((16, 88, 128), BF16),
            pltpu.VMEM((16, 80, 128), BF16),
            pltpu.VMEM((9 * C, C), BF16),
            pltpu.VMEM((C, C), BF16),
            pltpu.VMEM((C, C), BF16),
            pltpu.VMEM((128, C), F32),
            pltpu.VMEM((NZ, 2, SHARD, 128), F32),
            pltpu.VMEM((C, 128), BF16),
            pltpu.VMEM((128, C), BF16),
            pltpu.VMEM((PAIRS, 128, 256), BF16),
            pltpu.VMEM((PAIRS, 256, 128), BF16),
            pltpu.VMEM((STEPS + 1, TOK + 2 * COLS, 128), BF16),
            pltpu.VMEM((TOK + 2 * COLS, 3 * C), BF16),
            pltpu.VMEM((TOK, C), F32),
            pltpu.VMEM((TOK, C), F32),
            pltpu.VMEM((TOK, 128), F32),
            pltpu.VMEM((STEPS, TOK, 128), F32),
            pltpu.VMEM((STEPS, 128, TOK), BF16),
            pltpu.VMEM((TOK, C), BF16),
            pltpu.VMEM((128, C), F32),
            pltpu.VMEM((16, 8, 128), F32),
            pltpu.VMEM((16, 8, 128), F32),
            pltpu.VMEM((8, 128), F32),
            pltpu.VMEM((16, 8, 128), F32),
            dma((3, 8)),
            dma((3, 8)),
            dma((3, 4)),
            dma((3, 4)),
            dma((3, 4, 2, 4)),
            dma((3, 4, 2, 4)),
            dma((28,)),
            dma((28,)),
            dma((16,)),
            dma((16,)),
            dma((16,)),
            dma((16,)),
            dma((STEPS, 2)),
            dma((STEPS, 2)),
            dma((16,)),
            dma((16,)),
            dma((16,)),
            dma((16,)),
            dma,
        ],
        compiler_params=pltpu.CompilerParams(
            collective_id=0, has_side_effects=True, vmem_limit_bytes=58 * 1024 * 1024
        ),
        name="ddpo",
    )(
        latents.reshape(32, 128),
        noise.reshape(STEPS * 32, 128),
        rewards.reshape(1, 1),
        prompt_ids.reshape(1, 1),
        flat_context,
        time_bias,
        gain_first,
        gain_second,
        gain_third,
        w_in,
        w_conv.T,
        w_query,
        w_key.T,
        w_value.T,
        w_attn_out,
        w_final.T,
    )
    g = grad.T
    moment_one = 0.9 * moment_first + 0.1 * g
    moment_two = 0.999 * moment_second + 0.001 * g * g
    new_weight = w_final - learn_rate * moment_one / (jnp.sqrt(moment_two) + 1e-08)
    return (x_new.reshape(latents.shape), new_weight, moment_one, moment_two)


def solution(mesh):
    placed = (
        P("sec", None, "dev", None),
        P(None, "sec", None, "dev", None),
        P("sec"),
        P("sec"),
        P(),
        P(),
        P(),
        P(),
        P(),
        P("sec", "dev"),
        P("sec", "dev"),
        P("sec", "dev"),
        P("sec", "dev"),
        P("sec", "dev"),
        P("sec", "dev"),
        P("sec", "dev"),
        P("sec", "dev"),
        P("sec", "dev"),
    )
    return jax.shard_map(
        per_device,
        mesh=mesh,
        in_specs=placed,
        out_specs=(P("sec", None, "dev", None), P("sec", "dev"), P("sec", "dev"), P("sec", "dev")),
        check_vma=False,
    )
```

time: 149 us -> 123 us (0.83)
  local copies, waits for them, and re-layouts: 22.1 us -> 1.34 us
  Pallas kernels: 125 us -> 118 us
    unnamed x33 -> x7, local copies, waits for them, and re-layouts: 13.2 us -> 1.34 us
    pallas_call x1, Pallas kernels: 125 us -> 118 us  [per_device(): pl.pallas_call(body, out_shape=(jax.ShapeDtypeStruct((32, 128), F32), jax...]
    reshape x6 -> x0, local copies, waits for them, and re-layouts: 3.67 us -> none  [the longest x2 1.09 us: per_device(): blocks = x_new.reshape(4, 2, 2, ROWS, COLS)]
    transpose x2 -> x0, local copies, waits for them, and re-layouts: 3.08 us -> none  [to_features(): return blocks.transpose(0, 1, 3, 5, 2, 4).reshape(lead, FEAT, TOK)]
where the time goes in v2:
time: 123 us
  Pallas kernels  118 us (96%)
  between operations  2.01 us (2%)
  local copies, waits for them, and re-layouts  1.34 us (1%)
    pallas_call x1, Pallas kernels, per_device(): pl.pallas_call(body, out_shape=(jax.ShapeDtypeStruct((32, 128), F32), jax...  118 us

profile of v2, /device:TPU:1, one launch (start us, length us, event | category | flops | bytes accessed | tf_op | source)
XLA Modules:
  0.0 122.8 jit_solution(9450976928815837788)
XLA Ops:
  0.6 0.0 copy-start
  0.6 0.0 copy-start.2
  0.7 0.0 copy-start.1
  2.0 118.3 %ddpo.1 = (f32[32,128]{1,0:T(8,128)}, f32[1,40]{1,0:T(1,128)}) custom-call(f32[32,128]{1,0:T(8,128)} %bitcast.24, f32[192,128]{1,0:T(8,128)} %bitcast.22, f32[1,1]{1,0:T(1,128)} %bitcast.19.reward_ref, s32[1,1]{1,0:T(1,128)} %bitcast.20.prompt_ref, bf16[616,2048]{1,0:T(8,128)(2,1)} %bitcast.21, f32[6,640]{1,0:T(8,128)} %bias_ref.1, f32[640]{0:T(1024)} %g1_ref.1, ...), custom_call_target="tpu_custom_call" | custom-call | tf_op jit(solution)/shard_map/ddpo/pallas_call | solution.py:592
  120.3 0.0 copy-done
  120.3 0.0 copy-done.2
  120.3 0.0 copy-done.1
  120.3 1.1 divide_subtract_fusion
  121.5 1.3 %copy.25 = f32[1,4,8,128]{3,2,1,0:T(8,128)} copy(f32[1,4,8,128]{3,2,1,0:T(8,128)} %bitcast.25) | data formatting | bytes 32768
Async XLA Ops:
  0.6 119.7 %copy-start = (f32[40,1]{0,1:T(1,128)S(1)}, f32[40,1]{0,1:T(1,128)}, u32[]{:S(2)}) copy-start(f32[40,1]{0,1:T(1,128)} %param.33) | copy-start | bytes 484
  0.6 119.7 %copy-start.2 = (f32[40,1]{0,1:T(1,128)S(1)}, f32[40,1]{0,1:T(1,128)}, u32[]{:S(2)}) copy-start(f32[40,1]{0,1:T(1,128)} %param.35) | copy-start | bytes 484
  0.7 119.7 %copy-start.1 = (f32[40,1]{0,1:T(1,128)S(1)}, f32[40,1]{0,1:T(1,128)}, u32[]{:S(2)}) copy-start(f32[40,1]{0,1:T(1,128)} %param.34) | copy-start | bytes 484

commit v3 on v2

--- a/solution.py
+++ b/solution.py
@@ -100,6 +100,9 @@
     x_out,
     g_out,
     CX,
+    IN,
+    XO,
+    KO,
     G,
     KG,
     KT,
@@ -143,6 +146,8 @@
     r_recv,
     s_send,
     s_recv,
+    i_send,
+    i_recv,
     c_sem,
 ):
     sec = lax.axis_index("sec")
@@ -160,12 +165,26 @@
         pos[axis] = lax.rem(me[axis] + delta + SIZE[axis], SIZE[axis])
         return device(pos["x"], pos["y"], pos["z"], core)
 
+    image = 2 * z + yhi
+    pos = 2 * (xx + ylo * (7 - 2 * xx)) + core
+    column = 4 * xx + 2 * ylo + core
+
+    def worker(i, p):
+        place_q = p // 2
+        side = place_q // 4
+        return device(place_q + side * (7 - 2 * place_q), (i % 2) * 2 + side, i // 2, p % 2)
+
+    stays = jnp.logical_and(image == sec, pos == dev)
+
     barrier = pltpu.get_barrier_semaphore()
-    cross_y = (sec - 2 * ylo + 1, dev - 2 * yhi + 2 * (1 - yhi))
-    for k in range(1, 16):
-        pl.semaphore_signal(barrier, inc=1, device_id=(lax.rem(sec + k, 16), dev), device_id_type=MESH_ID)
-        pl.semaphore_signal(barrier, inc=1, device_id=(sec, lax.rem(dev + k, 16)), device_id_type=MESH_ID)
-    pl.semaphore_signal(barrier, inc=1, device_id=cross_y, device_id_type=MESH_ID)
+
+    def greet(peer):
+        pl.semaphore_signal(barrier, inc=1, device_id=peer, device_id_type=MESH_ID)
+
+    for i in range(1, NY * NZ):
+        greet(device(xx, lax.rem(yy + i // NZ, NY), lax.rem(z + i % NZ, NZ), core))
+    for i in range(1, 2 * NX * NY):
+        greet(device(lax.rem(xx + i // 8, NX), lax.rem(yy + (i // 2) % 4, NY), z, lax.rem(core + i % 2, 2)))
 
     context_copy = pltpu.make_async_copy(ctx_ref, CX, c_sem)
     context_copy.start()
@@ -206,42 +225,47 @@
         both = jnp.concatenate([cols[0:COLS], cols[COLS : 2 * COLS]], axis=1)
         return jnp.where(own_row, jnp.concatenate([both] * ROWS, axis=0), 0.0)
 
-    pl.semaphore_wait(barrier, 31)
+    pl.semaphore_wait(barrier, NY * NZ - 1 + 2 * NX * NY - 1)
 
     def halo_copy(t, up):
         if up:
-            src, dst, to, i = PB.at[t, pl.ds(COLS, COLS)], PB.at[t, pl.ds(COLS + TOK, COLS)], dev - 1, 0
+            src, dst, to, i = PB.at[t, pl.ds(COLS, COLS)], PB.at[t, pl.ds(COLS + TOK, COLS)], pos + 15, 0
         else:
-            src, dst, to, i = PB.at[t, pl.ds(TOK, COLS)], PB.at[t, pl.ds(0, COLS)], dev + 1, 1
+            src, dst, to, i = PB.at[t, pl.ds(TOK, COLS)], PB.at[t, pl.ds(0, COLS)], pos + 1, 1
         return pltpu.make_async_remote_copy(
-            src, dst, h_send.at[t, i], h_recv.at[t, i], device_id=(sec, to), device_id_type=MESH_ID
+            src, dst, h_send.at[t, i], h_recv.at[t, i], device_id=worker(image, lax.rem(to, 16)), device_id_type=MESH_ID
         )
 
     def start_halo(t):
-        @pl.when(dev > 0)
-        def _():
-            halo_copy(t, True).start()
-
-        @pl.when(dev < 15)
-        def _():
-            halo_copy(t, False).start()
+        halo_copy(t, True).start()
+        halo_copy(t, False).start()
 
     def wait_halo(t):
-        @pl.when(dev > 0)
-        def _():
-            halo_copy(t, True).wait_send()
-            halo_copy(t, False).wait_recv()
-
-        @pl.when(dev < 15)
-        def _():
-            halo_copy(t, False).wait_send()
-            halo_copy(t, True).wait_recv()
+        halo_copy(t, True).wait()
+        halo_copy(t, False).wait()
 
     def to_peer(src, dst, send, recv, peer):
         return pltpu.make_async_remote_copy(src, dst, send, recv, device_id=peer, device_id_type=MESH_ID)
 
+    def latents_in():
+        return to_peer(lat_ref, IN.at[pl.ds(0, 32)], i_send.at[0], i_recv.at[0], worker(sec, dev))
+
+    def noise_in():
+        return to_peer(noise_ref, IN.at[pl.ds(32, 32 * STEPS)], i_send.at[1], i_recv.at[1], worker(sec, dev))
+
+    def latents_out():
+        return to_peer(XO.at[0], XO.at[1], i_send.at[2], i_recv.at[2], (image, pos))
+
+    @pl.when(jnp.logical_not(stays))
+    def _():
+        latents_in().start()
+
     def key_copy(k):
-        return to_peer(KG.at[sec], KG.at[sec], k_send.at[k], k_recv.at[k], (lax.rem(sec + k, 16), dev))
+        peer = device(xx, lax.rem(yhi + k % 2, 2) * 2 + yhi, lax.rem(z + k // 2, NZ), core)
+        return to_peer(KO, KG.at[sec], k_send.at[k], k_recv.at[2 * (k // 2) + ylo], peer)
+
+    def key_arrival(i):
+        return to_peer(KO, KG.at[sec], k_send.at[0], k_recv.at[i], (sec, lax.rem(dev + 1, 16)))
 
     sent = []
     pushes = []
@@ -324,8 +348,8 @@
             yield
 
     def keys_and_values():
-        KG[sec, 0:SHARD, :] = w_key_ref[...]
-        KG[sec, SHARD : 2 * SHARD, :] = w_value_ref[...]
+        KO[0:SHARD, :] = w_key_ref[...]
+        KO[SHARD : 2 * SHARD, :] = w_value_ref[...]
         reward = jnp.broadcast_to(reward_ref[...], (8, 128))
         prompt = jnp.broadcast_to(prompt_ref[...].astype(F32), (8, 128))
         hi = reward.astype(BF16).astype(F32)
@@ -335,11 +359,20 @@
         stats = jnp.where(lane8 == 0, prompt, 0.0)
         for i, part in enumerate((hi, mid, low)):
             stats = jnp.where(lane8 == i + 1, part, stats)
-        KG[sec, 80:88, :] = stats.astype(BF16)
-        yield
-        yield
+        KO[80:88, :] = stats.astype(BF16)
         for k in range(1, 16):
             key_copy(k).start()
+
+        @pl.when(ylo != yhi)
+        def _():
+            key_copy(0).start()
+
+        @pl.when(ylo == yhi)
+        def _():
+            KG[sec] = KO[...]
+
+        yield
+        yield
         yield
         yield
         yield
@@ -347,16 +380,31 @@
         yield
         yield
         for k in range(1, 16):
-            key_copy(k).wait()
+            key_copy(k).wait_send()
+
+        @pl.when(ylo != yhi)
+        def _():
+            key_copy(0).wait_send()
+
+        for i in range(2, 16):
+            key_arrival(i).wait_recv()
+        key_arrival(1 - ylo).wait_recv()
+
+        @pl.when(ylo != yhi)
+        def _():
+            key_arrival(ylo).wait_recv()
+
         wide = jnp.concatenate([KG[s, 0:80, :] for s in range(16)], axis=1)
         context_copy.wait()
         every = dot_t(wide, CX[...]).astype(BF16)
         n = CX.shape[0]
-        mine = iota((n, 128), 0) == 8 * iota((n, 128), 1) + prompt_ref[...]
-        KT[dev] = dot(every, mine.astype(BF16)).astype(BF16)
+        own_prompt = KG[image, 80:88, :].astype(F32)[0:1, 0:1]
+        mine = (iota((n, 128), 0) - 8 * iota((n, 128), 1)).astype(F32) == own_prompt
+        KT[column] = dot(every, mine.astype(BF16)).astype(BF16)
 
         def copy(k):
-            return to_peer(KT.at[dev], KT.at[dev], t_send.at[k], t_recv.at[k], (sec, lax.rem(dev + k, 16)))
+            peer = worker(image, lax.rem(pos + k, 16))
+            return to_peer(KT.at[column], KT.at[column], t_send.at[k], t_recv.at[k], peer)
 
         for k in range(1, 16):
             copy(k).start()
@@ -382,19 +430,33 @@
             Vbd[p, 128:256, :] = jnp.where(lane < HEAD, 0.0, part).astype(BF16)
 
     def tokens():
+        @pl.when(jnp.logical_not(stays))
+        def _():
+            noise_in().start()
+            latents_in().wait()
+
+        @pl.when(stays)
+        def _():
+            IN[0:32, :] = lat_ref[...]
+            IN[32:, :] = noise_ref[...]
+
         X[...] = jnp.zeros_like(X)
-        X[:, 0:64] = turn(lat_ref[...])
+        X[:, 0:64] = turn(IN[0:32, :])
         PB[0, COLS : COLS + TOK, :] = X[...].astype(BF16)
         start_halo(0)
         yield
         yield
+        @pl.when(jnp.logical_not(stays))
+        def _():
+            noise_in().wait()
+
         GA[...] = jnp.zeros_like(GA)
         GS[...] = jnp.zeros_like(GS)
         Win[...] = jnp.zeros_like(Win)
         for t in range(STEPS):
             yield
             yield
-            nt = turn(noise_ref[32 * t : 32 * (t + 1), :])
+            nt = turn(IN[32 * (t + 1) : 32 * (t + 2), :])
             NZT[t] = jnp.concatenate([nt, jnp.zeros_like(nt)], axis=1)
             top = nt.astype(BF16).astype(F32)
             NTS[t] = jnp.transpose(jnp.concatenate([top, nt - top], axis=1)).astype(BF16)
@@ -445,10 +507,7 @@
     WI[...] = dot(by_row, Win[...].astype(BF16)).astype(BF16)
     valid = iota((TOK, 128), 0) // COLS == (iota((TOK, 128), 1) % 8) // 2
 
-    token_col = iota((TOK, C), 0) % COLS
-    tok_row = iota((2 * HEAD * 2, 2 * HEAD * 2), 0)
-    tok_col = iota((2 * HEAD * 2, 2 * HEAD * 2), 1)
-    ones = (((tok_row < 128) == (tok_col < 128)) & (tok_row % 128 < CTX_TOK)).astype(BF16)
+    real = iota((1, 128), 1) < CTX_TOK
 
     def spread(act, at, n):
         col = iota((n, C), 0) % COLS
@@ -467,33 +526,42 @@
         hidden = dot(PB[t, COLS : COLS + TOK, :], w_first) + bias
         H[...] = hidden
         spread(silu(rms(hidden, g1_ref[...].reshape(1, C))), COLS, TOK)
+        inner = TOK - COLS
         M[...] = H[...] + dot(A[COLS : COLS + TOK, :], Wc[3 * C : 6 * C, :])
+        M[COLS:TOK, :] += dot(A[COLS:TOK, :], Wc[0 : 3 * C, :])
         wait_halo(t)
+        M[0:inner, :] += dot(A[2 * COLS : COLS + TOK, :], Wc[6 * C : 9 * C, :])
         edge = jnp.concatenate([PB[t, 0:COLS, :], PB[t, COLS + TOK :, :]], axis=0)
         act = silu(rms(dot(edge, w_first) + bias, g1_ref[...].reshape(1, C)))
-        above = jnp.where(dev > 0, act[0:COLS], 0.0)
-        below = jnp.where(dev < 15, act[COLS:], 0.0)
+        above = jnp.where(pos > 0, act[0:COLS], 0.0)
+        below = jnp.where(pos < 15, act[COLS:], 0.0)
         spread(above, 0, COLS)
         spread(below, COLS + TOK, COLS)
-        M[...] += dot(A[0:TOK, :], Wc[0 : 3 * C, :])
-        M[...] += dot(A[2 * COLS : 2 * COLS + TOK, :], Wc[6 * C : 9 * C, :])
+        M[0:COLS, :] += dot(A[0:COLS, :], Wc[0 : 3 * C, :])
+        M[inner:TOK, :] += dot(A[COLS + TOK :, :], Wc[6 * C : 9 * C, :])
+
+        mixed = M[...]
+        normed = rms(mixed, g2_ref[...].reshape(1, C)).astype(BF16)
+        queries = dot(normed, Wq[...]).astype(BF16)
+        heads = []
+        for p in range(PAIRS):
+            e = jnp.exp(dot(queries[:, 128 * p : 128 * (p + 1)], Kbd[p]))
+            shares = []
+            for half in (e[:, 0:128], e[:, 128:256]):
+                total = jnp.sum(jnp.where(real, half, 0.0), axis=1, keepdims=True)
+                shares.append(half * (1.0 / total))
+            heads.append(dot(jnp.concatenate(shares, axis=1).astype(BF16), Vbd[p]).astype(BF16))
+        out = mixed + dot(jnp.concatenate(heads, axis=1), Wo[...])
 
         def finish(ranges):
+            def part(v):
+                return jnp.concatenate([v[a:b] for a, b in ranges], axis=0)
+
             def load(ref, *lead):
                 return jnp.concatenate([ref[(*lead, slice(a, b))] for a, b in ranges], axis=0)
 
-            mixed = load(M)
-            normed = rms(mixed, g2_ref[...].reshape(1, C)).astype(BF16)
-            queries = dot(normed, Wq[...]).astype(BF16)
-            heads = []
-            for p in range(PAIRS):
-                e = jnp.exp(dot(queries[:, 128 * p : 128 * (p + 1)], Kbd[p]))
-                total = dot(e.astype(BF16), ones)
-                heads.append(dot((e * (1.0 / total)).astype(BF16), Vbd[p]).astype(BF16))
-            out = mixed + dot(jnp.concatenate(heads, axis=1), Wo[...])
-            final = silu(rms(out, g3_ref[...].reshape(1, C))).astype(BF16)
-            keep = jnp.concatenate([valid[a:b] for a, b in ranges], axis=0)
-            predicted = jnp.where(keep, dot(final, WF[...]), 0.0)
+            final = silu(rms(part(out), g3_ref[...].reshape(1, C))).astype(BF16)
+            predicted = jnp.where(part(valid), dot(final, WF[...]), 0.0)
             x_new = scale * load(X) + beta * predicted + sigma * load(NZT, t)
             at = 0
             for a, b in ranges:
@@ -503,24 +571,28 @@
                 PB[t + 1, a + COLS : b + COLS, :] = x_new[at : at + n].astype(BF16)
                 at += n
 
-        finish(((0, TOK),))
+        finish(((0, COLS), (TOK - COLS, TOK)))
 
         @pl.when(t < STEPS - 1)
         def _():
             start_halo(t + 1)
 
+        finish(((COLS, TOK - COLS),))
         GA[...] += weight * dot(NTS[t], FA[...])
         return carry
 
     table = jnp.concatenate([KG[s, 80:88, :].astype(F32)[0:1] for s in range(16)], axis=0)
     ids = table[:, 0:1]
     rewards = table[:, 1:2] + table[:, 2:3] + table[:, 3:4]
-    same = jnp.where(ids == prompt_ref[...].astype(F32), 1.0, 0.0)
+    here = iota((16, 1), 0) == image
+    own_id = jnp.sum(jnp.where(here, ids, 0.0), axis=0, keepdims=True)
+    own_reward = jnp.sum(jnp.where(here, rewards, 0.0), axis=0, keepdims=True)
+    same = jnp.where(ids == own_id, 1.0, 0.0)
     count = jnp.maximum(jnp.sum(same, axis=0, keepdims=True), 1.0)
     mean = jnp.sum(same * rewards, axis=0, keepdims=True) / count
     square = jnp.sum(same * (rewards * rewards), axis=0, keepdims=True) / count
     spread_1 = jnp.sqrt(jnp.maximum(square - mean * mean, 1.0))
-    advantage = (reward_ref[...] - mean) / spread_1
+    advantage = (own_reward - mean) / spread_1
 
     lax.fori_loop(0, STEPS, denoise, 0)
 
@@ -541,9 +613,14 @@
     for r in range(1, ROWS):
         flat = flat + X[r * COLS : (r + 1) * COLS, 0:64]
     flat = jnp.concatenate([flat[:, 0:32], flat[:, 32:64]], axis=0)
-    x_out[...] = sum(
+    XO[0] = sum(
         lax.dot_general(part, pick, (((0,), (0,)), ((), ())), preferred_element_type=F32) for part in split(flat)
     )
+
+    @pl.when(jnp.logical_not(stays))
+    def _():
+        latents_out().start()
+
     for k in range(1, 16):
         column_copy(k).wait()
     R1[...] = jnp.sum(GR[...], axis=0)
@@ -562,6 +639,15 @@
     for j in range(5):
         hit = iota((128, 128), 1) + 128 * j == want
         picked = jnp.where(hit, jnp.broadcast_to(total[j : j + 1], (128, 128)), picked)
+    @pl.when(jnp.logical_not(stays))
+    def _():
+        latents_out().wait()
+        x_out[...] = XO[1]
+
+    @pl.when(stays)
+    def _():
+        x_out[...] = XO[0]
+
     g_out[...] = jnp.sum(jnp.transpose(picked), axis=0, keepdims=True)[:, 0:SHARD]
 
 
@@ -596,6 +682,9 @@
         out_specs=(vmem,) * 2,
         scratch_shapes=[
             pltpu.VMEM(flat_context.shape, BF16),
+            pltpu.VMEM((32 * (STEPS + 1), 128), F32),
+            pltpu.VMEM((2, 32, 128), F32),
+            pltpu.VMEM((88, 128), BF16),
             pltpu.VMEM((NZ, 2, NX, 2, 2, SHARD, LANES), BF16),
             pltpu.VMEM((16, 88, 128), BF16),
             pltpu.VMEM((16, 80, 128), BF16),
@@ -639,6 +728,8 @@
             dma((16,)),
             dma((16,)),
             dma((16,)),
+            dma((3,)),
+            dma((3,)),
             dma,
         ],
         compiler_params=pltpu.CompilerParams(

time: 123 us -> 116 us (0.943)
  Pallas kernels: 118 us -> 112 us
    pallas_call x1, Pallas kernels: 118 us -> 112 us  [per_device(): pl.pallas_call(body, out_shape=(jax.ShapeDtypeStruct((32, 128), F32), jax...]
where the time goes in v3:
time: 116 us
  Pallas kernels  112 us (97%)
  between operations  2.01 us (2%)
  local copies, waits for them, and re-layouts  1.34 us (1%)
    pallas_call x1, Pallas kernels, per_device(): pl.pallas_call(body, out_shape=(jax.ShapeDtypeStruct((32, 128), F32), jax...  112 us

profile of v3, /device:TPU:1, one launch (start us, length us, event | category | flops | bytes accessed | tf_op | source)
XLA Modules:
  0.0 116.0 jit_solution(15450511200792102386)
XLA Ops:
  0.6 0.0 copy-start
  0.6 0.0 copy-start.2
  0.7 0.0 copy-start.1
  2.0 111.6 %ddpo.1 = (f32[32,128]{1,0:T(8,128)}, f32[1,40]{1,0:T(1,128)}) custom-call(f32[32,128]{1,0:T(8,128)} %bitcast.24, f32[192,128]{1,0:T(8,128)} %bitcast.22, f32[1,1]{1,0:T(1,128)} %bitcast.19.reward_ref, s32[1,1]{1,0:T(1,128)} %bitcast.20.prompt_ref, bf16[616,2048]{1,0:T(8,128)(2,1)} %bitcast.21, f32[6,640]{1,0:T(8,128)} %bias_ref.1, f32[640]{0:T(1024)} %g1_ref.1, ...), custom_call_target="tpu_custom_call" | custom-call | tf_op jit(solution)/shard_map/ddpo/pallas_call | solution.py:678
  113.5 0.0 copy-done
  113.6 0.0 copy-done.2
  113.6 0.0 copy-done.1
  113.6 1.1 divide_subtract_fusion
  114.7 1.3 %copy.25 = f32[1,4,8,128]{3,2,1,0:T(8,128)} copy(f32[1,4,8,128]{3,2,1,0:T(8,128)} %bitcast.25) | data formatting | bytes 32768
Async XLA Ops:
  0.6 112.9 %copy-start = (f32[40,1]{0,1:T(1,128)S(1)}, f32[40,1]{0,1:T(1,128)}, u32[]{:S(2)}) copy-start(f32[40,1]{0,1:T(1,128)} %param.33) | copy-start | bytes 484
  0.6 112.9 %copy-start.2 = (f32[40,1]{0,1:T(1,128)S(1)}, f32[40,1]{0,1:T(1,128)}, u32[]{:S(2)}) copy-start(f32[40,1]{0,1:T(1,128)} %param.35) | copy-start | bytes 484
  0.7 112.9 %copy-start.1 = (f32[40,1]{0,1:T(1,128)S(1)}, f32[40,1]{0,1:T(1,128)}, u32[]{:S(2)}) copy-start(f32[40,1]{0,1:T(1,128)} %param.34) | copy-start | bytes 484

commit v4 on v3

--- a/solution.py
+++ b/solution.py
@@ -117,7 +117,6 @@
     Vbd,
     PB,
     A,
-    H,
     M,
     X,
     NZT,
@@ -396,11 +395,13 @@
 
         wide = jnp.concatenate([KG[s, 0:80, :] for s in range(16)], axis=1)
         context_copy.wait()
-        every = dot_t(wide, CX[...]).astype(BF16)
+        every = dot_t(CX[...], wide).astype(BF16)
         n = CX.shape[0]
         own_prompt = KG[image, 80:88, :].astype(F32)[0:1, 0:1]
-        mine = (iota((n, 128), 0) - 8 * iota((n, 128), 1)).astype(F32) == own_prompt
-        KT[column] = dot(every, mine.astype(BF16)).astype(BF16)
+        mine = (iota((128, n), 1) - 8 * iota((128, n), 0)).astype(F32) == own_prompt
+        own = dot(mine.astype(BF16), every)
+        own = jnp.concatenate([own, jnp.zeros((128, 48), F32)], axis=1)
+        KT[column] = jnp.transpose(own)[0:80].astype(BF16)
 
         def copy(k):
             peer = worker(image, lax.rem(pos + k, 16))
@@ -524,13 +525,10 @@
         bias = bias_ref[pl.ds(t, 1), :]
         w_first = WI[...]
         hidden = dot(PB[t, COLS : COLS + TOK, :], w_first) + bias
-        H[...] = hidden
         spread(silu(rms(hidden, g1_ref[...].reshape(1, C))), COLS, TOK)
-        inner = TOK - COLS
-        M[...] = H[...] + dot(A[COLS : COLS + TOK, :], Wc[3 * C : 6 * C, :])
+        M[...] = hidden + dot(A[COLS : COLS + TOK, :], Wc[3 * C : 6 * C, :])
         M[COLS:TOK, :] += dot(A[COLS:TOK, :], Wc[0 : 3 * C, :])
         wait_halo(t)
-        M[0:inner, :] += dot(A[2 * COLS : COLS + TOK, :], Wc[6 * C : 9 * C, :])
         edge = jnp.concatenate([PB[t, 0:COLS, :], PB[t, COLS + TOK :, :]], axis=0)
         act = silu(rms(dot(edge, w_first) + bias, g1_ref[...].reshape(1, C)))
         above = jnp.where(pos > 0, act[0:COLS], 0.0)
@@ -538,7 +536,7 @@
         spread(above, 0, COLS)
         spread(below, COLS + TOK, COLS)
         M[0:COLS, :] += dot(A[0:COLS, :], Wc[0 : 3 * C, :])
-        M[inner:TOK, :] += dot(A[COLS + TOK :, :], Wc[6 * C : 9 * C, :])
+        M[...] += dot(A[2 * COLS :, :], Wc[6 * C : 9 * C, :])
 
         mixed = M[...]
         normed = rms(mixed, g2_ref[...].reshape(1, C)).astype(BF16)
@@ -699,7 +697,6 @@
             pltpu.VMEM((PAIRS, 256, 128), BF16),
             pltpu.VMEM((STEPS + 1, TOK + 2 * COLS, 128), BF16),
             pltpu.VMEM((TOK + 2 * COLS, 3 * C), BF16),
-            pltpu.VMEM((TOK, C), F32),
             pltpu.VMEM((TOK, C), F32),
             pltpu.VMEM((TOK, 128), F32),
             pltpu.VMEM((STEPS, TOK, 128), F32),

time: 116 us -> 115 us (level)
  Pallas kernels: 112 us -> 110 us
    pallas_call x1, Pallas kernels: 112 us -> 110 us  [per_device(): pl.pallas_call(body, out_shape=(jax.ShapeDtypeStruct((32, 128), F32), jax...]
where the time goes in v4:
time: 115 us
  Pallas kernels  110 us (96%)
  between operations  2.01 us (2%)
  local copies, waits for them, and re-layouts  1.34 us (1%)
    pallas_call x1, Pallas kernels, per_device(): pl.pallas_call(body, out_shape=(jax.ShapeDtypeStruct((32, 128), F32), jax...  110 us

profile of v4, /device:TPU:1, one launch (start us, length us, event | category | flops | bytes accessed | tf_op | source)
XLA Modules:
  0.0 114.8 jit_solution(14432323504135124635)
XLA Ops:
  0.6 0.0 copy-start
  0.6 0.0 copy-start.2
  0.7 0.0 copy-start.1
  2.0 110.3 %ddpo.1 = (f32[32,128]{1,0:T(8,128)}, f32[1,40]{1,0:T(1,128)}) custom-call(f32[32,128]{1,0:T(8,128)} %bitcast.24, f32[192,128]{1,0:T(8,128)} %bitcast.22, f32[1,1]{1,0:T(1,128)} %bitcast.19.reward_ref, s32[1,1]{1,0:T(1,128)} %bitcast.20.prompt_ref, bf16[616,2048]{1,0:T(8,128)(2,1)} %bitcast.21, f32[6,640]{1,0:T(8,128)} %bias_ref.1, f32[640]{0:T(1024)} %g1_ref.1, ...), custom_call_target="tpu_custom_call" | custom-call | tf_op jit(solution)/shard_map/ddpo/pallas_call | solution.py:676
  112.3 0.0 copy-done
  112.3 0.0 copy-done.2
  112.3 0.0 copy-done.1
  112.4 1.1 divide_subtract_fusion
  113.5 1.3 %copy.25 = f32[1,4,8,128]{3,2,1,0:T(8,128)} copy(f32[1,4,8,128]{3,2,1,0:T(8,128)} %bitcast.25) | data formatting | bytes 32768
Async XLA Ops:
  0.6 111.7 %copy-start = (f32[40,1]{0,1:T(1,128)S(1)}, f32[40,1]{0,1:T(1,128)}, u32[]{:S(2)}) copy-start(f32[40,1]{0,1:T(1,128)} %param.33) | copy-start | bytes 484
  0.6 111.7 %copy-start.2 = (f32[40,1]{0,1:T(1,128)S(1)}, f32[40,1]{0,1:T(1,128)}, u32[]{:S(2)}) copy-start(f32[40,1]{0,1:T(1,128)} %param.35) | copy-start | bytes 484
  0.7 111.7 %copy-start.1 = (f32[40,1]{0,1:T(1,128)S(1)}, f32[40,1]{0,1:T(1,128)}, u32[]{:S(2)}) copy-start(f32[40,1]{0,1:T(1,128)} %param.34) | copy-start | bytes 484
